TPU v7x, 32 devices: a whole 2x2x4 slice. The times are simulated.
32 devices in a mesh: dp: 8 (over z, x), mp: 4 (over y, core).
Axes of the slice: x: 2, y: 2, z: 4, core: 2. Of those that a mesh axis runs over, the one named last changes fastest.
Arguments:
- images: bfloat16 [128, 52, 768], P('dp'), may hold values from -6 to 6
- ln1_gain: bfloat16 [768], replicated, may hold values from 0.5 to 1.5
- ln1_bias: bfloat16 [768], replicated, may hold values from -1 to 1
- w_qkv: bfloat16 [768, 3, 768], P(None, None, 'mp'), may hold values from -0.21875 to 0.21875
- qv_bias: bfloat16 [2, 768], P(None, 'mp'), may hold values from -1 to 1
- w_out: bfloat16 [768, 768], P('mp'), may hold values from -0.625 to 0.625
- out_bias: bfloat16 [768], replicated, may hold values from -1 to 1
- ln2_gain: bfloat16 [768], replicated, may hold values from 0.5 to 1.5
- ln2_bias: bfloat16 [768], replicated, may hold values from -1 to 1
- w_fc1: bfloat16 [768, 3072], P(None, 'mp'), may hold values from -0.21875 to 0.21875
- fc1_bias: bfloat16 [3072], P('mp'), may hold values from -1.5 to 1.5
- w_fc2: bfloat16 [3072, 768], P('mp'), may hold values from -0.15625 to 0.15625
- fc2_bias: bfloat16 [768], replicated, may hold values from -1 to 1
- post_gain: float32 [768], replicated, may hold values from 0.5 to 1.5
- post_bias: float32 [768], replicated, may hold values from -1 to 1
- w_proj: float32 [768, 512], replicated, may hold values from -0.21875 to 0.21875
- captions: float32 [384, 512], P('dp'), may hold values from 0.01 to 0.1
- logit_scale: float32 [1], replicated, may hold values from 3 to 3.7
- caption_counts: int32 [128], P('dp'), may hold values from 1 to 5, as said below
- positives: int32 [128, 5], P('dp'), may hold values from -1 to 383, as said below
Outputs:
- loss: float32 [1], replicated
- block_out: bfloat16 [128, 52, 768], P('dp')
- images_grad: float32 [128, 52, 768], P('dp')
- ln1_gain_grad: float32 [768], replicated
- ln1_bias_grad: float32 [768], replicated
- w_qkv_grad: float32 [768, 3, 768], P(None, None, 'mp')
- qv_bias_grad: float32 [2, 768], P(None, 'mp')
- w_out_grad: float32 [768, 768], P('mp')
- out_bias_grad: float32 [768], replicated
- ln2_gain_grad: float32 [768], replicated
- ln2_bias_grad: float32 [768], replicated
- w_fc1_grad: float32 [768, 3072], P(None, 'mp')
- fc1_bias_grad: float32 [3072], P('mp')
- w_fc2_grad: float32 [3072, 768], P('mp')
- fc2_bias_grad: float32 [768], replicated
- post_gain_grad: float32 [768], replicated
- post_bias_grad: float32 [768], replicated
- w_proj_grad: float32 [768, 512], replicated
- captions_grad: float32 [384, 512], P('dp')
- logit_scale_grad: float32 [1], replicated
Inputs may be any that keep to these rules, and one draw needn't show every extreme that they name: `caption_counts`: the counts of all images sum to 384. `positives`: row i names the distinct captions of image i in its first caption_counts[i] places and holds -1 in the rest; every caption belongs to exactly one image.
All inputs are finite; a program needn't handle non-finite values.
Results may differ from a plain program's by a relative error of at most 0.03.
Values may be sent and summed in bfloat16 or wider, within the bound.
A program may use at most 128 MiB of HBM per device.

v0:
```python
import jax
import jax.numpy as jnp
from jax import lax
from jax.sharding import PartitionSpec as P

HEAD_DIM = 64


HIGH = lax.Precision.HIGHEST


def merged(x, axis, join):
    gathered = jax.tree.map(
        lambda a, kind: lax.all_gather(a.astype(kind), axis),
        x,
        (jnp.bfloat16, jnp.bfloat16, jnp.bfloat16),
    )

    def take(source):
        return jax.tree.map(
            lambda a, own: lax.dynamic_index_in_dim(a, source, 0, False).astype(own.dtype),
            gathered,
            x,
        )

    return lax.fori_loop(
        1, lax.axis_size(axis), lambda source, state: join(state, take(source)), take(0)
    )


def split_up(x, dim, peers):
    dims = x.shape
    tiles = x.reshape(*dims[:dim], peers, dims[dim] // peers, *dims[dim + 1 :])
    return jnp.moveaxis(tiles, dim, 0)


def sum_at_owner(x, axis, dim):
    peers = lax.axis_size(axis)
    tiles = lax.all_to_all(split_up(x, dim, peers), axis, 0, 0, tiled=True)
    return jnp.sum(tiles.astype(jnp.float32), axis=0)


def norm_rows(values, gain, shift):
    centre = values - jnp.mean(values, -1, keepdims=True)
    spread = lax.rsqrt(jnp.mean(centre * centre, -1, keepdims=True) + 1e-05)
    scaled = centre * spread
    return (scaled * gain + shift, scaled, spread)


def norm_back(upper, gain, scaled, spread):
    inner = upper * gain
    lower = spread * (
        inner
        - jnp.mean(inner, -1, keepdims=True)
        - scaled * jnp.mean(inner * scaled, -1, keepdims=True)
    )
    return (lower, jnp.sum(upper * scaled, 0), jnp.sum(upper, 0))


def unit_rows(values):
    factor = lax.rsqrt(jnp.sum(values * values, -1, keepdims=True) + 1e-06)
    return (values * factor, factor)


def unit_back(upper, unit, factor):
    return factor * (upper - unit * jnp.sum(unit * upper, -1, keepdims=True))


def combine_stats(first, second):
    top = jnp.maximum(first[0], second[0])
    total = first[1] * jnp.exp(first[0] - top) + second[1] * jnp.exp(second[0] - top)
    return (top, total, first[2] + second[2])


def contract_rows(left, right, precision=None):
    return lax.dot_general(
        left,
        right,
        (((0,), (0,)), ((), ())),
        precision=precision,
        preferred_element_type=jnp.float32,
    )


def contract_cols(left, right, precision=None):
    return lax.dot_general(
        left,
        right,
        (((1,), (1,)), ((), ())),
        precision=precision,
        preferred_element_type=jnp.float32,
    )


def body(
    images,
    ln1_gain,
    ln1_bias,
    w_qkv,
    qv_bias,
    w_out,
    out_bias,
    ln2_gain,
    ln2_bias,
    w_fc1,
    fc1_bias,
    w_fc2,
    fc2_bias,
    post_gain,
    post_bias,
    w_proj,
    captions,
    logit_scale,
    caption_counts,
    positives,
):
    image_count, seq_len, model_width = images.shape
    row_count = image_count * seq_len
    local_width = w_qkv.shape[2]
    head_count = local_width // HEAD_DIM

    def first_rows(values):
        return values.reshape(image_count, seq_len, -1)[:, 0]

    inputs = images.astype(jnp.float32).reshape(row_count, model_width)
    gain_one = ln1_gain.astype(jnp.float32)
    shift_one = ln1_bias.astype(jnp.float32)
    gain_two = ln2_gain.astype(jnp.float32)
    shift_two = ln2_bias.astype(jnp.float32)
    normed_one, scaled_one, spread_one = norm_rows(inputs, gain_one, shift_one)
    attn_in = normed_one.astype(jnp.bfloat16)
    qkv_flat = w_qkv.reshape(model_width, 3 * local_width)
    projected = jnp.dot(attn_in, qkv_flat, preferred_element_type=jnp.float32).reshape(
        row_count, 3, local_width
    )
    bias_pair = qv_bias.astype(jnp.float32)
    head_shape = (image_count, seq_len, head_count, HEAD_DIM)
    queries = (projected[:, 0] + bias_pair[0]).astype(jnp.bfloat16).reshape(head_shape)
    keys_all = projected[:, 1].astype(jnp.bfloat16).reshape(head_shape)
    values_all = (projected[:, 2] + bias_pair[1]).astype(jnp.bfloat16).reshape(head_shape)
    scores = (
        jnp.einsum("gqhe,gkhe->ghqk", queries, keys_all, preferred_element_type=jnp.float32) * 0.125
    )
    probs = jax.nn.softmax(scores, -1)
    probs_low = probs.astype(jnp.bfloat16)
    context = jnp.einsum(
        "ghqk,gkhe->gqhe", probs_low, values_all, preferred_element_type=jnp.float32
    )
    context = context.reshape(row_count, local_width).astype(jnp.bfloat16)
    attn_out = lax.psum(jnp.dot(context, w_out, preferred_element_type=jnp.float32), "mp")
    middle = inputs + attn_out + out_bias.astype(jnp.float32)
    normed_two, scaled_two, spread_two = norm_rows(middle, gain_two, shift_two)
    mlp_in = normed_two.astype(jnp.bfloat16)
    pre_act = jnp.dot(mlp_in, w_fc1, preferred_element_type=jnp.float32) + fc1_bias.astype(
        jnp.float32
    )
    sigma = jax.nn.sigmoid(1.702 * pre_act)
    activated = (pre_act * sigma).astype(jnp.bfloat16)
    mlp_out = lax.psum(
        jnp.dot(activated, w_fc2, preferred_element_type=jnp.float32).astype(jnp.bfloat16), "mp"
    ).astype(jnp.float32)
    result = middle + mlp_out + fc2_bias.astype(jnp.float32)
    block_out = result.astype(jnp.bfloat16).reshape(image_count, seq_len, model_width)
    cls_rows = first_rows(result)
    scaled_cls = first_rows(scaled_two)
    spread_cls = first_rows(spread_two)
    mlp_in_cls = first_rows(mlp_in)
    pre_cls = first_rows(pre_act)
    sigma_cls = first_rows(sigma)
    act_cls = first_rows(activated)
    post_normed, post_scaled, post_spread = norm_rows(cls_rows, post_gain, post_bias)
    embedded = jnp.dot(post_normed, w_proj, precision=HIGH)
    image_unit, image_factor = unit_rows(embedded)
    image_low = image_unit.astype(jnp.bfloat16)
    text_unit, text_factor = unit_rows(captions)
    text_low = text_unit.astype(jnp.bfloat16)
    scale = jnp.exp(logit_scale[0])
    counts_float = caption_counts.astype(jnp.float32)
    cap_dev = captions.shape[0]
    dp_size = lax.axis_size("dp")
    image_total = image_count * dp_size
    caption_total = cap_dev * dp_size
    dp_index = lax.axis_index("dp")
    text_all = lax.all_gather(text_low, "dp", axis=0, tiled=True)
    cosine = contract_cols(image_low, text_all)
    logits = scale * cosine
    caption_ids = lax.iota(jnp.int32, caption_total)
    matches = jnp.any(positives[:, :, None] == caption_ids[None, None, :], axis=1).astype(
        jnp.float32
    )
    row_top = jnp.max(logits, 1, keepdims=True)
    row_lse = row_top + jnp.log(jnp.sum(jnp.exp(logits - row_top), 1, keepdims=True))
    col_top = jnp.max(logits, 0)
    col_total = jnp.sum(jnp.exp(logits - col_top[None, :]), 0)
    col_match = jnp.sum(matches * logits, 0)
    glob_top, glob_total, glob_match = merged((col_top, col_total, col_match), "dp", combine_stats)
    col_lse = glob_top + jnp.log(glob_total)
    text_terms = lax.dynamic_slice_in_dim(col_lse - glob_match, dp_index * cap_dev, cap_dev)
    image_terms = row_lse[:, 0] - jnp.sum(matches * logits, 1) / counts_float
    loss_part = 0.5 * jnp.sum(image_terms) / image_total + 0.5 * jnp.sum(text_terms) / caption_total
    logit_grad = 0.5 / image_total * (
        jnp.exp(logits - row_lse) - matches / counts_float[:, None]
    ) + 0.5 / caption_total * (jnp.exp(logits - col_lse[None, :]) - matches)
    grad_low = logit_grad.astype(jnp.bfloat16)
    image_grad = scale * jnp.dot(grad_low, text_all, preferred_element_type=jnp.float32)
    text_grad = sum_at_owner(
        (scale * contract_rows(grad_low, image_low)).astype(jnp.bfloat16), "dp", 0
    )
    scale_part = jnp.sum(grad_low.astype(jnp.float32) * cosine)
    captions_grad = unit_back(text_grad, text_unit, text_factor)
    embed_grad = unit_back(image_grad, image_unit, image_factor)
    proj_grad = contract_rows(post_normed, embed_grad, HIGH)
    post_upper = contract_cols(embed_grad, w_proj, HIGH)
    cls_grad, post_gain_grad, post_bias_grad = norm_back(
        post_upper, post_gain, post_scaled, post_spread
    )
    out_grad_low = cls_grad.astype(jnp.bfloat16)
    fc2_bias_grad = jnp.sum(cls_grad, 0)
    fc2_grad = contract_rows(act_cls, out_grad_low)
    act_grad = contract_cols(out_grad_low, w_fc2)
    pre_grad = (act_grad * (sigma_cls + 1.702 * pre_cls * sigma_cls * (1.0 - sigma_cls))).astype(
        jnp.bfloat16
    )
    fc1_bias_grad = jnp.sum(pre_grad.astype(jnp.float32), 0)
    fc1_grad = contract_rows(mlp_in_cls, pre_grad)
    norm_upper = lax.psum(contract_cols(pre_grad, w_fc1).astype(jnp.bfloat16), "mp").astype(
        jnp.float32
    )
    mid_part, gain_two_grad, shift_two_grad = norm_back(
        norm_upper, gain_two, scaled_cls, spread_cls
    )
    mid_grad = cls_grad + mid_part
    mid_low = mid_grad.astype(jnp.bfloat16)
    out_bias_grad = jnp.sum(mid_grad, 0)
    out_weight_grad = contract_rows(first_rows(context), mid_low)
    context_grad = (
        contract_cols(mid_low, w_out)
        .astype(jnp.bfloat16)
        .reshape(image_count, head_count, HEAD_DIM)
    )
    first_probs = probs[:, :, 0, :]
    prob_grad = jnp.einsum(
        "ghe,gkhe->ghk", context_grad, values_all, preferred_element_type=jnp.float32
    )
    score_grad = (
        first_probs * (prob_grad - jnp.sum(first_probs * prob_grad, -1, keepdims=True))
    ).astype(jnp.bfloat16)
    query_first = queries[:, 0]
    query_grad = (
        0.125
        * jnp.einsum("ghk,gkhe->ghe", score_grad, keys_all, preferred_element_type=jnp.float32)
    ).astype(jnp.bfloat16)
    key_grad = (
        0.125
        * jnp.einsum("ghk,ghe->gkhe", score_grad, query_first, preferred_element_type=jnp.float32)
    ).astype(jnp.bfloat16)
    value_grad = jnp.einsum(
        "ghk,ghe->gkhe", probs_low[:, :, 0, :], context_grad, preferred_element_type=jnp.float32
    ).astype(jnp.bfloat16)
    query_full = jnp.pad(query_grad[:, None], ((0, 0), (0, seq_len - 1), (0, 0), (0, 0)))
    qkv_rows = jnp.stack([query_full, key_grad, value_grad], 2).reshape(row_count, 3 * local_width)
    qkv_grad = contract_rows(attn_in, qkv_rows).reshape(model_width, 3, local_width)
    bias_grad = jnp.stack(
        [
            jnp.sum(query_grad.astype(jnp.float32), 0).reshape(local_width),
            jnp.sum(value_grad.astype(jnp.float32), (0, 1)).reshape(local_width),
        ]
    )
    norm_lower = lax.psum(contract_cols(qkv_rows, qkv_flat).astype(jnp.bfloat16), "mp").astype(
        jnp.float32
    )
    input_part, gain_one_grad, shift_one_grad = norm_back(
        norm_lower, gain_one, scaled_one, spread_one
    )
    residual_rows = jnp.pad(mid_grad[:, None], ((0, 0), (0, seq_len - 1), (0, 0))).reshape(
        row_count, model_width
    )
    images_grad = (input_part + residual_rows).reshape(image_count, seq_len, model_width)
    summed = lax.psum(
        (
            fc1_grad,
            fc1_bias_grad,
            fc2_grad,
            fc2_bias_grad,
            gain_two_grad,
            shift_two_grad,
            post_gain_grad,
            post_bias_grad,
            proj_grad,
            loss_part,
            scale_part,
            qkv_grad,
            bias_grad,
            out_weight_grad,
            out_bias_grad,
            gain_one_grad,
            shift_one_grad,
        ),
        "dp",
    )
    late_sums = summed[:11]
    early_sums = summed[11:]
    loss = late_sums[9].reshape(1)
    scale_grad = (late_sums[10] * scale).reshape(1)
    return (
        loss,
        block_out,
        images_grad,
        early_sums[4],
        early_sums[5],
        early_sums[0],
        early_sums[1],
        early_sums[2],
        early_sums[3],
        late_sums[4],
        late_sums[5],
        late_sums[0],
        late_sums[1],
        late_sums[2],
        late_sums[3],
        late_sums[6],
        late_sums[7],
        late_sums[8],
        captions_grad,
        scale_grad,
    )


def solution(mesh):
    return jax.shard_map(
        body,
        mesh=mesh,
        in_specs=(
            P("dp", None, None),
            P(),
            P(),
            P(None, None, "mp"),
            P(None, "mp"),
            P("mp", None),
            P(),
            P(),
            P(),
            P(None, "mp"),
            P("mp"),
            P("mp", None),
            P(),
            P(),
            P(),
            P(),
            P("dp", None),
            P(),
            P("dp"),
            P("dp", None),
        ),
        out_specs=(
            P(),
            P("dp", None, None),
            P("dp", None, None),
            P(),
            P(),
            P(None, None, "mp"),
            P(None, "mp"),
            P("mp", None),
            P(),
            P(),
            P(),
            P(None, "mp"),
            P("mp"),
            P("mp", None),
            P(),
            P(),
            P(),
            P(),
            P("dp", None),
            P(),
        ),
        check_vma=False,
    )
```

profile of v0, /device:TPU:0, one launch (start us, length us, event | category | flops | bytes accessed | tf_op | source)
XLA Modules:
  0.0 659.1 jit_solution(6171423924685881486)
XLA Ops:
  23.7 3.6 squeeze.63
  27.3 3.3 copy.181
  51.0 3.1 fusion.91
  61.5 54.4 %all-reduce.9.cloned.1.call-done = f32[832,768]{1,0:T(8,128)} async-done(((f32[832,768]{1,0:T(8,128)}), f32[832,768]{1,0:T(8,128)}) %all-reduce.9.cloned.1.call-update) | async-done | bytes 2555920 | tf_op jit(solution)/shard_map/psum | solution.py:150
  121.5 3.6 add_divide_fusion
  136.9 31.3 %all_gather.15 = bf16[384,512]{1,0:T(8,128)(2,1)S(1)} all-gather(bf16[48,512]{1,0:T(8,128)(2,1)} %multiply_convert_fusion.3), channel_id=1, replica_groups=mesh['dp'=8,'mp'=4] {'dp'}, dimensions={0}, use_global_device_ids=true | all-gather | bytes 442368 | tf_op jit(solution)/shard_map/all_gather | solution.py:184
  178.7 3.0 reshape.348
  190.1 4.4 fusion.81
  194.5 3.0 reshape.345
  200.6 25.9 %all-gather.4 = bf16[8,1,384]{2,1,0:T(2,128)(2,1)S(1)} all-gather(bf16[1,1,384]{2,1,0:T(2,128)(2,1)S(1)} %reshape.383), channel_id=3, replica_groups=mesh['dp'=8,'mp'=4] {'dp'}, dimensions={0}, use_global_device_ids=true | all-gather | bytes 6912 | tf_op jit(solution)/shard_map/all_gather | solution.py:14
  226.5 25.9 %all-gather.3 = bf16[8,1,384]{2,1,0:T(2,128)(2,1)S(1)} all-gather(bf16[1,1,384]{2,1,0:T(2,128)(2,1)S(1)} %reshape.381), channel_id=2, replica_groups=mesh['dp'=8,'mp'=4] {'dp'}, dimensions={0}, use_global_device_ids=true | all-gather | bytes 6912 | tf_op jit(solution)/shard_map/all_gather | solution.py:14
  252.5 25.9 %all-gather.5 = bf16[8,1,384]{2,1,0:T(2,128)(2,1)S(1)} all-gather(bf16[1,1,384]{2,1,0:T(2,128)(2,1)S(1)} %reshape.385), channel_id=4, replica_groups=mesh['dp'=8,'mp'=4] {'dp'}, dimensions={0}, use_global_device_ids=true | all-gather | bytes 6912 | tf_op jit(solution)/shard_map/all_gather | solution.py:14
  289.0 11.4 %psum.150 = bf16[16,768]{1,0:T(8,128)(2,1)S(1)} all-reduce(bf16[16,768]{1,0:T(8,128)(2,1)} %convolution_convert_fusion.3), channel_id=1, replica_groups=mesh['dp'=8,'mp'=4] {'mp'}, use_global_device_ids=true, to_apply=%region_27.28 | all-reduce | flops 12288 | bytes 49152 | tf_op jit(solution)/shard_map/psum | solution.py:226
  307.4 4.0 copy.195
  311.4 4.0 reshape.354
  315.5 3.4 convolution_convert_fusion.1
  331.6 3.5 all-to-all-start
  343.2 10.4 %all-reduce.13.cloned.1.call-done = bf16[832,768]{1,0:T(8,128)(2,1)} async-done(((bf16[832,768]{1,0:T(8,128)(2,1)}), bf16[832,768]{1,0:T(8,128)(2,1)}) %all-reduce.13.cloned.1.call-update) | async-done | bytes 1277968 | tf_op jit(solution)/shard_map/psum | solution.py:269
  353.6 3.4 fusion.9
  357.1 41.6 %all-reduce.2 = (f32[1]{0:T(128)}, f32[768]{0:T(1024)}, f32[768]{0:T(1024)}, f32[2,192]{1,0:T(2,128)}, f32[768]{0:T(1024)}, /*index=5*/f32[768]{0:T(1024)}, f32[...) all-reduce(f32[1]{0:T(128)} %bitcast.6, ...), channel_id=1, replica_groups=mesh['dp'=8,'mp'=4] {'dp'}, use_global_device_ids=true, to_apply=%region_23.24 | all-reduce | flops 7298 | bytes 58384 | tf_op jit(solution)/shard_map/psum | solution.py:279
  399.3 4.0 fusion.7
  403.4 3.0 reshape.356
  406.4 4.4 copy.199
  411.8 229.5 %all-reduce.15.cloned.1.call-done = (f32[768,3,192]{0,2,1:T(8,128)}, f32[192,768]{1,0:T(8,128)}, f32[768,768]{1,0:T(8,128)}, f32[768,768]{1,0:T(8,128)}, f32[768,512]{1,0:T(8,128)}) async-done(((f32[768,3,192]{0,2,1:T(8,128)}, f32[192,768]{1,0:T(8,128)}, f32[768,768]{1,0:T(8,128)}, f32[768,768]{1,0:T(8,128)}, f32[768,512]{1,0:T(8,128)}), (f32[768,3,192]{0,2,1:T(8,128)}, f32[192,768]{1,0:T(8,128)}, ...) | async-done | bytes 8650768 | tf_op jit(solution)/shard_map/psum | solution.py:279
  (324 shorter events, 130.7 us)
Async XLA Ops:
  7.2 191.8 %copy-start = (f32[768,512]{1,0:T(8,128)S(1)}, f32[768,512]{1,0:T(8,128)}, u32[]{:S(2)}) copy-start(f32[768,512]{1,0:T(8,128)} %param.37) | copy-start | bytes 4718596
  7.2 108.6 %all-reduce.9.cloned.1.call-start = ((), (), s32[]{:S(2)}) async-start(), calls=%async_computation.1 | async-start | bytes 5111808 | tf_op jit(solution)/shard_map/psum | solution.py:150
  54.1 136.0 %all-reduce.11.cloned.1.call-start = ((), (), s32[]{:S(2)}) async-start(), calls=%async_computation.2 | async-start | bytes 2555904 | tf_op jit(solution)/shard_map/psum | solution.py:159
  56.4 62.8 %copy-start.45 = (f32[768]{0:T(1024)}, f32[768]{0:T(1024)S(1)}, u32[]{:S(2)}) copy-start(f32[768]{0:T(1024)S(1)} %convert_element_type.268) | copy-start | bytes 9220
  60.8 58.0 %copy-start.61 = (f32[48]{0:T(128)}, f32[48]{0:T(128)S(1)}, u32[]{:S(2)}) copy-start(f32[48]{0:T(128)S(1)} %add_rsqrt_fusion.2) | copy-start | bytes 580
  128.4 41.2 %copy-start.48 = (f32[832]{0:T(1024)S(1)}, f32[832]{0:T(1024)}, u32[]{:S(2)}) copy-start(f32[832]{0:T(1024)} %copy-done.47) | copy-start | bytes 9988
  128.4 225.2 %all-reduce.13.cloned.1.call-start = ((), (), s32[]{:S(2)}) async-start(), calls=%async_computation.3 | async-start | bytes 2555904 | tf_op jit(solution)/shard_map/psum | solution.py:269
  134.6 172.0 %copy-start.23 = (f32[16,3,52]{0,1,2:T(4,128)}, f32[16,3,52]{0,1,2:T(4,128)S(1)}, u32[]{:S(2)}) copy-start(f32[16,3,52]{0,1,2:T(4,128)S(1)} %copy.194) | copy-start | bytes 29956
  177.1 123.2 %copy-start.30 = (f32[16,1,768]{2,1,0:T(1,128)}, f32[16,1,768]{2,1,0:T(1,128)S(1)}, u32[]{:S(2)}) copy-start(f32[16,1,768]{2,1,0:T(1,128)S(1)} %slice.87) | copy-start | bytes 147460
  197.5 81.7 %copy-start.72 = (s32[16]{0:T(128)S(1)}, s32[16]{0:T(128)}, u32[]{:S(2)}) copy-start(s32[16]{0:T(128)} %param.40) | copy-start | bytes 196
  197.5 82.9 %copy-start.71 = (f32[16]{0:T(128)S(1)}, f32[16]{0:T(128)}, u32[]{:S(2)}) copy-start(f32[16]{0:T(128)} %convert_element_type.278) | copy-start | bytes 196
  200.0 86.1 %copy-start.58 = (f32[16]{0:T(128)}, f32[16]{0:T(128)S(1)}, u32[]{:S(2)}) copy-start(f32[16]{0:T(128)S(1)} %add_rsqrt_fusion.3) | copy-start | bytes 196
  283.4 16.9 %copy-start.46 = (f32[768]{0:T(1024)S(1)}, f32[768]{0:T(1024)}, u32[]{:S(2)}) copy-start(f32[768]{0:T(1024)} %copy-done.45) | copy-start | bytes 9220
  283.4 17.5 %copy-start.65 = (f32[16]{0:T(128)S(1)}, f32[16]{0:T(128)}, u32[]{:S(2)}) copy-start(f32[16]{0:T(128)} %slice_reduce_fusion) | copy-start | bytes 196
  286.1 16.4 %copy-start.18 = (bf16[192,768]{1,0:T(8,128)(2,1)S(1)}, bf16[192,768]{1,0:T(8,128)(2,1)}, u32[]{:S(2)}) copy-start(bf16[192,768]{1,0:T(8,128)(2,1)} %param.27) | copy-start | bytes 884740
  286.1 16.8 %copy-start.9 = (bf16[16,52,3,64]{3,1,2,0:T(8,128)(2,1)S(1)}, bf16[16,52,3,64]{3,1,2,0:T(8,128)(2,1)}, u32[]{:S(2)}) copy-start(bf16[16,52,3,64]{3,1,2,0:T(8,128)(2,1)} %copy.185) | copy-start | bytes 958468
  286.8 16.5 %copy-start.27 = (f32[16,768]{1,0:T(8,128)}, f32[16,768]{1,0:T(8,128)S(1)}, u32[]{:S(2)}) copy-start(f32[16,768]{1,0:T(8,128)S(1)} %get-tuple-element.397) | copy-start | bytes 147460
  286.8 17.6 %copy-start.7 = (bf16[16,52,3,64]{3,1,2,0:T(8,128)(2,1)S(1)}, bf16[16,52,3,64]{3,1,2,0:T(8,128)(2,1)}, u32[]{:S(2)}) copy-start(bf16[16,52,3,64]{3,1,2,0:T(8,128)(2,1)} %copy-done.6) | copy-start | bytes 958468
  287.9 17.5 %copy-start.32 = (bf16[16,768]{1,0:T(8,128)(2,1)}, bf16[16,768]{1,0:T(8,128)(2,1)S(1)}, u32[]{:S(2)}) copy-start(bf16[16,768]{1,0:T(8,128)(2,1)S(1)} %get-tuple-element.431) | copy-start | bytes 73732
  319.0 322.3 %all-reduce.15.cloned.1.call-start = ((), (), s32[]{:S(2)}) async-start(), calls=%async_computation.4 | async-start | bytes 17301504 | tf_op jit(solution)/shard_map/psum | solution.py:279
  331.6 79.1 %all-to-all-start = ((bf16[8,48,512]{2,1,0:T(8,128)(2,1)}), bf16[8,48,512]{2,1,0:T(8,128)(2,1)S(1)}, u32[]{:S(2)}, u32[]{:S(2)}) async-start(bf16[8,48,512]{2,1,0:T(8,128)(2,1)} %bitcast.26), calls=%async_computation | async-start | bytes 786432 | tf_op jit(solution)/shard_map/all_to_all | solution.py:39
  337.5 16.2 %copy-start.44 = (f32[768]{0:T(1024)S(1)}, f32[768]{0:T(1024)}, u32[]{:S(2)}) copy-start(f32[768]{0:T(1024)} %copy-done.43) | copy-start | bytes 9220
  343.1 13.9 %copy-start.50 = (f32[768]{0:T(1024)S(1)}, f32[768]{0:T(1024)}, u32[]{:S(2)}) copy-start(f32[768]{0:T(1024)} %get-tuple-element.345) | copy-start | bytes 9220
  353.6 45.7 %copy-start.3 = (bf16[832,768]{1,0:T(8,128)(2,1)S(1)}, bf16[832,768]{1,0:T(8,128)(2,1)}, u32[]{:S(2)}) copy-start(bf16[832,768]{1,0:T(8,128)(2,1)} %all-reduce.13.cloned.1.call-done) | copy-start | bytes 3833860
  (54 other events, 248.1 us)
Sparse Core Ops, SparseCore 0:
  54.3 61.5 all-reduce.8
  128.5 38.5 all-reduce.10
  319.1 34.5 all-reduce.12
  361.0 280.2 all-reduce.14
where the time goes:
time: 669 us; the launch traced here: 659 us
  waiting for transfers between devices  294 us (44%)
  blocking collectives  162 us (24%)
  local copies, waits for them, and re-layouts  95.2 us (14%)
  other arithmetic  50.3 us (8%)
  matrix products  34.4 us (5%)
  between operations  18.9 us (3%)
    psum x1, waiting for transfers between devices, body(): lax.psum((fc1_grad, fc1_bias_grad, fc2_grad, fc2_bias_grad, gain_two_grad...  230 us
    all_gather x3, blocking collectives, merged(): lax.all_gather(a.astype(kind), axis)  77.7 us
    psum x1, waiting for transfers between devices, body(): lax.psum(jnp.dot(context, w_out, preferred_element_type=jnp.float32), 'mp')  54.4 us
    psum x1, blocking collectives, body(): lax.psum((fc1_grad, fc1_bias_grad, fc2_grad, fc2_bias_grad, gain_two_grad...  41.6 us
    all_gather x1, blocking collectives, body(): text_all = lax.all_gather(text_low, 'dp', axis=0, tiled=True)  31.3 us
    unnamed x160, local copies, waits for them, and re-layouts  18.4 us
    reshape x6, local copies, waits for them, and re-layouts, first_rows(): return values.reshape(image_count, seq_len, -1)[:, 0]  15.3 us
  transfers between devices with their start and end apart: 5, of which 3 were waited for; matrix products, arithmetic and copies ran while one was open for 11% of the time, Pallas kernels for 0%

commit v1 on v0

v1 whole, which is shorter than its diff:
```python
import jax
import jax.numpy as jnp
from jax import lax
from jax.sharding import PartitionSpec as P

HEAD_DIM = 64
HIGH = lax.Precision.HIGHEST
F32 = jnp.float32
BF16 = jnp.bfloat16


def norm_rows(values, gain, shift):
    centre = values - jnp.mean(values, -1, keepdims=True)
    spread = lax.rsqrt(jnp.mean(centre * centre, -1, keepdims=True) + 1e-05)
    scaled = centre * spread
    return (scaled * gain + shift, scaled, spread)


def norm_back(upper, gain, scaled, spread):
    inner = upper * gain
    return spread * (
        inner
        - jnp.mean(inner, -1, keepdims=True)
        - scaled * jnp.mean(inner * scaled, -1, keepdims=True)
    )


def dot(a, b, ca=1, cb=0, precision=None):
    return lax.dot_general(
        a, b, (((ca,), (cb,)), ((), ())), precision=precision, preferred_element_type=F32
    )


def gather_dp(x):
    return lax.all_gather(x, "dp", axis=0, tiled=True)


def gather_mp(x):
    return lax.all_gather(x, "mp", axis=0, tiled=True)


def sum_mp(x):
    return lax.psum(x, "mp")


def body(
    images,
    ln1_gain,
    ln1_bias,
    w_qkv,
    qv_bias,
    w_out,
    out_bias,
    ln2_gain,
    ln2_bias,
    w_fc1,
    fc1_bias,
    w_fc2,
    fc2_bias,
    post_gain,
    post_bias,
    w_proj,
    captions,
    logit_scale,
    caption_counts,
    positives,
):
    group, seq, width = images.shape
    rows = group * seq
    local = w_qkv.shape[2]
    heads = local // HEAD_DIM
    dp = lax.axis_index("dp")
    image_total = group * lax.axis_size("dp")
    cap_own = captions.shape[0]
    caption_total = cap_own * lax.axis_size("dp")

    x = jnp.transpose(images, (1, 0, 2)).reshape(rows, width).astype(F32)
    wt = jnp.transpose(w_qkv, (1, 2, 0)).reshape(3 * local, width)
    g1, b1, g2, b2 = (v.astype(F32) for v in (ln1_gain, ln1_bias, ln2_gain, ln2_bias))
    attn_f, xhat, spread1 = norm_rows(x, g1, b1)
    attn_in = attn_f.astype(BF16)
    bias = qv_bias.astype(F32)
    q = (dot(attn_in, wt[:local], 1, 1) + bias[0]).astype(BF16)
    k = dot(attn_in, wt[local : 2 * local], 1, 1).astype(BF16)
    v = (dot(attn_in, wt[2 * local :], 1, 1) + bias[1]).astype(BF16)

    lane_head = lax.broadcasted_iota(jnp.int32, (heads, group, local), 2) // HEAD_DIM
    own_head = lane_head == lax.broadcasted_iota(jnp.int32, (heads, group, local), 0)
    own_head = own_head.reshape(heads * group, local)

    def spread_heads(t):
        return jnp.where(own_head, jnp.tile(t, (heads, 1)), 0)

    def join_heads(t):
        return jnp.sum(jnp.where(own_head, t, 0).reshape(heads, group, local), 0)

    hg = heads * group
    same = (
        lax.broadcasted_iota(jnp.int32, (hg, rows), 0) % group
        == lax.broadcasted_iota(jnp.int32, (hg, rows), 1) % group
    )
    q_cls = q[:group]
    qx = spread_heads(q_cls)
    scores = jnp.where(same, dot(qx, k, 1, 1) * 0.125, -jnp.inf)
    probs = jax.nn.softmax(scores, -1)
    probs_low = probs.astype(BF16)
    ctx_cls = join_heads(dot(probs_low, v)).astype(BF16)
    b_rows = dot(probs_low, attn_in).astype(BF16)
    prob_sum = jnp.sum(probs_low.astype(F32), -1, keepdims=True)

    def grouped(t):
        return jnp.transpose(t.reshape(seq, group, heads, HEAD_DIM), (1, 2, 0, 3))

    sc = jnp.einsum("ghqe,ghke->ghqk", grouped(q), grouped(k), preferred_element_type=F32) * 0.125
    pr = jax.nn.softmax(sc, -1).astype(BF16)
    ctx = jnp.einsum("ghqk,ghke->ghqe", pr, grouped(v), preferred_element_type=F32)
    ctx = jnp.transpose(ctx, (2, 0, 1, 3)).reshape(rows, local).astype(BF16)

    x_cls = gather_dp(images[:, 0])
    text_unit_own_factor = lax.rsqrt(jnp.sum(captions * captions, -1, keepdims=True) + 1e-06)
    text_unit = captions * text_unit_own_factor
    text_low = gather_dp(text_unit.astype(BF16))
    plan = gather_dp(jnp.concatenate([positives, caption_counts[:, None]], 1))
    w_out_all = gather_mp(w_out)
    ctx_mine = gather_dp(ctx_cls)
    ctx_all = lax.all_gather(ctx_mine, "mp", axis=1, tiled=True)
    middle = x_cls.astype(F32) + dot(ctx_all, w_out_all) + out_bias.astype(F32)
    norm2, xhat2, spread2 = norm_rows(middle, g2, b2)
    mlp_in = norm2.astype(BF16)
    pre = dot(mlp_in, w_fc1) + fc1_bias.astype(F32)
    sigma = jax.nn.sigmoid(1.702 * pre)
    act = (pre * sigma).astype(BF16)
    y = middle + sum_mp(dot(act, w_fc2).astype(BF16)).astype(F32) + fc2_bias.astype(F32)

    ctx_full = lax.all_gather(ctx, "mp", axis=1, tiled=True)
    mid_bulk = x + dot(ctx_full, w_out_all) + out_bias.astype(F32)
    in_bulk = norm_rows(mid_bulk, g2, b2)[0].astype(BF16)
    pre_bulk = dot(in_bulk, w_fc1) + fc1_bias.astype(F32)
    act_bulk = (pre_bulk * jax.nn.sigmoid(1.702 * pre_bulk)).astype(BF16)
    out_bulk = sum_mp(dot(act_bulk, w_fc2).astype(BF16)).astype(F32)
    block_out = (mid_bulk + out_bulk + fc2_bias.astype(F32)).astype(BF16)

    post, post_hat, post_spread = norm_rows(y, post_gain, post_bias)
    emb = dot(post, w_proj, precision=HIGH)
    factor = lax.rsqrt(jnp.sum(emb * emb, -1, keepdims=True) + 1e-06)
    unit = emb * factor
    image_low = unit.astype(BF16)
    scale = jnp.exp(logit_scale[0])
    cosine = dot(image_low, text_low, 1, 1)
    logits = scale * cosine
    ids = lax.broadcasted_iota(jnp.int32, (image_total, caption_total), 1)
    match = jnp.zeros((image_total, caption_total), jnp.bool_)
    for place in range(positives.shape[1]):
        match |= plan[:, place : place + 1] == ids
    match = match.astype(F32)
    counts = plan[:, positives.shape[1] :].astype(F32)
    row_lse = jax.nn.logsumexp(logits, 1, keepdims=True)
    col_lse = jax.nn.logsumexp(logits, 0, keepdims=True)
    matched = match * logits
    loss = 0.5 / image_total * jnp.sum(
        row_lse - jnp.sum(matched, 1, keepdims=True) / counts
    ) + 0.5 / caption_total * jnp.sum(col_lse - jnp.sum(matched, 0, keepdims=True))
    dlog = 0.5 / image_total * (jnp.exp(logits - row_lse) - match / counts)
    dlog += 0.5 / caption_total * (jnp.exp(logits - col_lse) - match)
    dlog = dlog.astype(BF16)
    scale_grad = scale * jnp.sum(dlog.astype(F32) * cosine)
    dimage = scale * dot(dlog, text_low)
    dtext = scale * dot(dlog, image_low, 0, 0)
    dtext = lax.dynamic_slice_in_dim(dtext, dp * cap_own, cap_own)
    captions_grad = text_unit_own_factor * (
        dtext - text_unit * jnp.sum(text_unit * dtext, -1, keepdims=True)
    )
    demb = factor * (dimage - unit * jnp.sum(unit * dimage, -1, keepdims=True))
    proj_grad = dot(post, demb, 0, 0, HIGH)
    dpost = dot(demb, w_proj, 1, 1, HIGH)
    dcls = norm_back(dpost, post_gain, post_hat, post_spread)
    dy = dcls.astype(BF16)
    fc2_grad = dot(act, dy, 0, 0)
    dpre = dot(dy, w_fc2, 1, 1) * (sigma + 1.702 * pre * sigma * (1.0 - sigma))
    dpre = dpre.astype(BF16)
    fc1_grad = dot(mlp_in, dpre, 0, 0)
    dmlp = sum_mp(dot(dpre, w_fc1, 1, 1).astype(BF16)).astype(F32)
    dmid = dcls + norm_back(dmlp, g2, xhat2, spread2)
    dmid_low = dmid.astype(BF16)
    out_grad = dot(ctx_mine, dmid_low, 0, 0)
    dctx = dot(dmid_low, w_out, 1, 1).astype(BF16)

    dctx_own = lax.dynamic_slice_in_dim(dctx, dp * group, group)
    dmid_own = lax.dynamic_slice_in_dim(dmid, dp * group, group)
    dx = spread_heads(dctx_own)
    dprobs = dot(dx, v, 1, 1)
    dscores = probs * (dprobs - jnp.sum(probs * dprobs, -1, keepdims=True))
    dscores = (dscores * 0.125).astype(BF16)
    dq = join_heads(dot(dscores, k)).astype(BF16)
    a_rows = dot(dscores, attn_in).astype(BF16)
    u_k = dot(qx, wt[local : 2 * local]).astype(BF16)
    u_v = dot(dx, wt[2 * local :]).astype(BF16)
    u_q = dot(dq, wt[:local]).astype(BF16)
    fold = (
        lax.broadcasted_iota(jnp.int32, (rows, seq), 0) // group
        == lax.broadcasted_iota(jnp.int32, (rows, seq), 1)
    ).astype(BF16)
    coef = dot(jnp.concatenate([dscores, probs_low], 0), fold).astype(BF16)
    u_all = gather_mp(jnp.concatenate([u_k, u_v], 0))
    c_all = gather_mp(coef)
    q_all = jnp.sum(gather_mp(u_q).reshape(-1, group, width).astype(F32), 0)
    ct = dot(fold, c_all, 1, 1)
    ct = jnp.where(
        lax.broadcasted_iota(jnp.int32, ct.shape, 0) % group
        == lax.broadcasted_iota(jnp.int32, ct.shape, 1) % group,
        ct,
        0,
    ).astype(BF16)
    dattn = dot(ct, u_all)
    dattn = jnp.concatenate([dattn[:group] + q_all, dattn[group:]], 0)
    back1 = norm_back(dattn, g1, xhat, spread1)
    images_grad = jnp.concatenate([back1[:group] + dmid_own, back1[group:]], 0)

    a_all = gather_dp(a_rows)
    b_all = gather_dp(b_rows)
    dq_all = gather_dp(dq)
    qx_all = gather_dp(qx)
    dx_all = gather_dp(dx)
    attn_cls = norm_rows(x_cls.astype(F32), g1, b1)[0].astype(BF16)
    wq_grad = dot(dq_all, attn_cls, 0, 0)
    wk_grad = dot(qx_all, a_all, 0, 0)
    wv_grad = dot(dx_all, b_all, 0, 0)
    qkv_grad = jnp.concatenate([wq_grad, wk_grad, wv_grad], 0)
    qkv_grad = jnp.transpose(qkv_grad.reshape(3, local, width), (2, 0, 1))
    small = lax.psum(
        (
            jnp.sum(dattn * xhat, 0),
            jnp.sum(dattn, 0),
            jnp.stack(
                [jnp.sum(dq.astype(F32), 0), jnp.sum(dx.astype(F32) * prob_sum, 0)]
            ),
        ),
        "dp",
    )

    def as_images(t):
        return jnp.transpose(t.reshape(seq, group, width), (1, 0, 2))

    return (
        loss.reshape(1),
        as_images(block_out),
        as_images(images_grad),
        small[0],
        small[1],
        qkv_grad,
        small[2],
        out_grad,
        jnp.sum(dmid, 0),
        jnp.sum(dmlp * xhat2, 0),
        jnp.sum(dmlp, 0),
        fc1_grad,
        jnp.sum(dpre.astype(F32), 0),
        fc2_grad,
        jnp.sum(dcls, 0),
        jnp.sum(dpost * post_hat, 0),
        jnp.sum(dpost, 0),
        proj_grad,
        captions_grad,
        scale_grad.reshape(1),
    )


def solution(mesh):
    full, per_dp = P(), P("dp")
    return jax.shard_map(
        body,
        mesh=mesh,
        in_specs=(
            P("dp", None, None),
            full,
            full,
            P(None, None, "mp"),
            P(None, "mp"),
            P("mp", None),
            full,
            full,
            full,
            P(None, "mp"),
            P("mp"),
            P("mp", None),
            full,
            full,
            full,
            full,
            P("dp", None),
            full,
            per_dp,
            P("dp", None),
        ),
        out_specs=(
            full,
            P("dp", None, None),
            P("dp", None, None),
            full,
            full,
            P(None, None, "mp"),
            P(None, "mp"),
            P("mp", None),
            full,
            full,
            full,
            P(None, "mp"),
            P("mp"),
            P("mp", None),
            full,
            full,
            full,
            full,
            P("dp", None),
            full,
        ),
        check_vma=False,
    )
```

time: 669 us -> 517 us (0.77); the launches traced: 659 us -> 516 us
  waiting for transfers between devices: 294 us -> 36.5 us
  blocking collectives: 162 us -> 343 us
  local copies, waits for them, and re-layouts: 95.2 us -> 16.6 us
  matrix products: 34.4 us -> 57.1 us
  other arithmetic: 50.3 us -> 42.1 us
    psum x4 -> x2, waiting for transfers between devices: 294 us -> 35.8 us  [sum_mp(): return lax.psum(x, 'mp')]
    all_gather x4 -> x13, blocking collectives: 109 us -> 306 us  [the longest x9 282 us: gather_dp(): return lax.all_gather(x, 'dp', axis=0, tiled=True)]
    reshape x13 -> x3, local copies, waits for them, and re-layouts: 29.9 us -> 2.52 us  [grouped(): return jnp.transpose(t.reshape(seq, group, heads, HEAD_DIM), (1, 2, 0, 3))]
    dot_general x22 -> x36, matrix products: 34.4 us -> 54.5 us  [the longest x34 46.9 us: dot(): lax.dot_general(a, b, (((ca,), (cb,)), ((), ())), precision=precision, pr...]
    psum x2 -> x1, blocking collectives: 52.9 us -> 37 us  [body(): lax.psum((jnp.sum(dattn * xhat, 0), jnp.sum(dattn, 0), jnp.stack([jnp.sum...]
    convert_element_type x10 -> x7, local copies, waits for them, and re-layouts: 20.6 us -> 5.75 us  [the longest x3 3.09 us: body(): ctx = jnp.transpose(ctx, (2, 0, 1, 3)).reshape(rows, local).astype(BF16)]
    unnamed x160 -> x238, local copies, waits for them, and re-layouts: 18.4 us -> 4.3 us
    convert_element_type x34 -> x12, other arithmetic: 19.4 us -> 6.73 us  [the longest x2 2.96 us: body(): attn_in = attn_f.astype(BF16)]
  transfers between devices with their start and end apart: 5 -> 4, of which waited for: 3 -> 1; matrix products, arithmetic and copies ran while one was open for 11% -> 12% of each run, Pallas kernels for 0% -> 0%
where the time goes in v1:
time: 517 us; the launch traced here: 516 us
  blocking collectives  343 us (66%)
  matrix products  57.1 us (11%)
  other arithmetic  42.1 us (8%)
  waiting for transfers between devices  36.5 us (7%)
  between operations  20.3 us (4%)
  local copies, waits for them, and re-layouts  16.6 us (3%)
    all_gather x9, blocking collectives, gather_dp(): return lax.all_gather(x, 'dp', axis=0, tiled=True)  282 us
    dot_general x34, matrix products, dot(): lax.dot_general(a, b, (((ca,), (cb,)), ((), ())), precision=precision, pr...  46.9 us
    psum x1, blocking collectives, body(): lax.psum((jnp.sum(dattn * xhat, 0), jnp.sum(dattn, 0), jnp.stack([jnp.sum...  37 us
    psum x2, waiting for transfers between devices, sum_mp(): return lax.psum(x, 'mp')  35.8 us
    all_gather x3, blocking collectives, gather_mp(): return lax.all_gather(x, 'mp', axis=0, tiled=True)  18.2 us
  transfers between devices with their start and end apart: 4, of which 1 were waited for; matrix products, arithmetic and copies ran while one was open for 12% of the time, Pallas kernels for 0%

profile of v1, /device:TPU:0, one launch (start us, length us, event | category | flops | bytes accessed | tf_op | source)
XLA Modules:
  0.0 516.0 jit_solution(3807066683726582704)
XLA Ops:
  21.5 32.4 %all_gather.46 = bf16[128,192]{1,0:T(8,128)(2,1)S(1)} all-gather(bf16[16,192]{1,0:T(8,128)(2,1)S(1)} %reduce_sum.416), channel_id=1, replica_groups=mesh['dp'=8,'mp'=4] {'dp'}, dimensions={0}, use_global_device_ids=true | all-gather | bytes 55296 | tf_op jit(solution)/shard_map/all_gather | solution.py:35
  57.0 6.0 %all_gather.47 = bf16[128,768]{0,1:T(8,128)(2,1)} all-gather(bf16[128,192]{0,1:T(8,128)(2,1)S(1)} %copy.83), channel_id=1, replica_groups=mesh['dp'=8,'mp'=4] {'mp'}, dimensions={1}, use_global_device_ids=true | all-gather | bytes 245760 | tf_op jit(solution)/shard_map/all_gather | solution.py:126
  63.0 30.7 %all-gather = bf16[128,1,768]{2,0,1:T(8,128)(2,1)S(1)} all-gather(bf16[16,1,768]{2,0,1:T(8,128)(2,1)S(1)} %slice-done), channel_id=2, replica_groups=mesh['dp'=8,'mp'=4] {'dp'}, dimensions={0}, use_global_device_ids=true | all-gather | bytes 221184 | tf_op jit(solution)/shard_map/all_gather | solution.py:35
  96.4 3.8 convolution_multiply_fusion
  104.7 3.7 fusion.28
  116.7 32.8 %all_gather.56 = bf16[384,192]{1,0:T(8,128)(2,1)} all-gather(bf16[48,192]{1,0:T(8,128)(2,1)} %copy-done.43), channel_id=1, replica_groups=mesh['dp'=8,'mp'=4] {'dp'}, dimensions={0}, use_global_device_ids=true | all-gather | bytes 165888 | tf_op jit(solution)/shard_map/all_gather | solution.py:35
  150.5 31.0 %all_gather.49 = bf16[384,512]{1,0:T(8,128)(2,1)S(1)} all-gather(bf16[48,512]{1,0:T(8,128)(2,1)S(1)} %multiply_convert_fusion.4), channel_id=1, replica_groups=mesh['dp'=8,'mp'=4] {'dp'}, dimensions={0}, use_global_device_ids=true | all-gather | bytes 442368 | tf_op jit(solution)/shard_map/all_gather | solution.py:35
  182.9 30.6 %all-gather.1 = s32[8,16,6]{1,2,0:T(8,128)S(1)} all-gather(s32[1,16,6]{1,2,0:T(8,128)S(1)} %add_bitcast_fusion), channel_id=1, replica_groups=mesh['dp'=8,'mp'=4] {'dp'}, dimensions={0}, use_global_device_ids=true | all-gather | bytes 3456 | tf_op jit(solution)/shard_map/all_gather | solution.py:35
  227.6 3.4 multiply_reduce_fusion.2
  235.1 2.7 fusion.62
  237.8 2.9 bitcast_add_fusion
  242.9 6.0 %convolution_convert_fusion = bf16[832,768]{1,0:T(8,128)(2,1)} fusion(bf16[768,768]{1,0:T(8,128)(2,1)} %param.31, bf16[768,768]{1,0:T(8,128)(2,1)} %param.29, f32[832,768]{1,0:T(8,128)} %copy-done.3, f32[768]{0:T(1024)} %copy-done.66, f32[768]{0:T(1024)S(1)} %copy-done.60, f32[768]{0:T(1024)S(1)} %convert_element_type.228, f32[832]{0:T(1024)} %add_rsqrt_fusion.1, ...), kind=kOutput, calls=%fused_computation.33 | convolution fusion | flops 1971879936 | bytes 6212096 | tf_op jit(solution)/shard_map/dot_general | solution.py:29
  250.6 2.9 fusion.140
  255.7 35.8 %all-reduce.7.cloned.1.call-done = (bf16[832,768]{1,0:T(8,128)(2,1)}, bf16[128,768]{1,0:T(8,128)(2,1)}) async-done(((bf16[832,768]{1,0:T(8,128)(2,1)}, bf16[128,768]{1,0:T(8,128)(2,1)}), (bf16[832,768]{1,0:T(8,128)(2,1)}, bf16[128,768]{1,0:T(8,128)(2,1)})) %all-reduce.7.cloned.1.call-update) | async-done | bytes 1474576 | tf_op jit(solution)/shard_map/psum | solution.py:43
  298.6 7.6 %all_gather.53 = bf16[384,768]{1,0:T(8,128)(2,1)} all-gather(bf16[96,768]{1,0:T(8,128)(2,1)S(1)} %pad_maximum_fusion.3), channel_id=1, replica_groups=mesh['dp'=8,'mp'=4] {'mp'}, dimensions={0}, use_global_device_ids=true | all-gather | bytes 737280 | tf_op jit(solution)/shard_map/all_gather | solution.py:39
  307.8 5.3 %all-gather.2 = bf16[4,96,52]{1,2,0:T(8,128)(2,1)S(1)} all-gather(bf16[1,96,52]{1,2,0:T(8,128)(2,1)S(1)} %fusion.35), channel_id=1, replica_groups=mesh['dp'=8,'mp'=4] {'mp'}, dimensions={0}, use_global_device_ids=true | all-gather | bytes 49920 | tf_op jit(solution)/shard_map/all_gather | solution.py:39
  313.2 3.9 fusion.29
  317.1 4.0 slice_reduce_fusion
  322.2 5.3 %all_gather.54 = bf16[64,768]{1,0:T(8,128)(2,1)S(1)} all-gather(bf16[16,768]{1,0:T(8,128)(2,1)S(1)} %convolution_convert_fusion.9), channel_id=1, replica_groups=mesh['dp'=8,'mp'=4] {'mp'}, dimensions={0}, use_global_device_ids=true | all-gather | bytes 122880 | tf_op jit(solution)/shard_map/all_gather | solution.py:39
  336.3 30.9 %all_gather.58 = bf16[384,192]{1,0:T(8,128)(2,1)S(1)} all-gather(bf16[48,192]{1,0:T(8,128)(2,1)S(1)} %copy-done.45), channel_id=1, replica_groups=mesh['dp'=8,'mp'=4] {'dp'}, dimensions={0}, use_global_device_ids=true | all-gather | bytes 165888 | tf_op jit(solution)/shard_map/all_gather | solution.py:35
  367.8 30.6 %all_gather.55 = bf16[128,192]{1,0:T(8,128)(2,1)S(1)} all-gather(bf16[16,192]{1,0:T(8,128)(2,1)S(1)} %reduce_sum.438), channel_id=1, replica_groups=mesh['dp'=8,'mp'=4] {'dp'}, dimensions={0}, use_global_device_ids=true | all-gather | bytes 55296 | tf_op jit(solution)/shard_map/all_gather | solution.py:35
  401.2 31.7 %all_gather.59 = bf16[384,768]{1,0:T(8,128)(2,1)S(1)} all-gather(bf16[48,768]{1,0:T(8,128)(2,1)S(1)} %convolution_convert_fusion.5), channel_id=1, replica_groups=mesh['dp'=8,'mp'=4] {'dp'}, dimensions={0}, use_global_device_ids=true | all-gather | bytes 663552 | tf_op jit(solution)/shard_map/all_gather | solution.py:35
  432.9 31.3 %all_gather.57 = bf16[384,768]{1,0:T(8,128)(2,1)S(1)} all-gather(bf16[48,768]{1,0:T(8,128)(2,1)S(1)} %convolution_convert_fusion.6), channel_id=1, replica_groups=mesh['dp'=8,'mp'=4] {'dp'}, dimensions={0}, use_global_device_ids=true | all-gather | bytes 663552 | tf_op jit(solution)/shard_map/all_gather | solution.py:35
  467.8 37.0 %all-reduce = (f32[768]{0:T(1024)}, f32[768]{0:T(1024)}, f32[2,192]{1,0:T(2,128)}) all-reduce(f32[768]{0:T(1024)S(1)} %copy-done.67, f32[768]{0:T(1024)S(1)} %reduce_sum.445, f32[2,192]{1,0:T(2,128)S(1)} %pad_maximum_fusion.4), channel_id=1, replica_groups=mesh['dp'=8,'mp'=4] {'dp'}, use_global_device_ids=true, to_apply=%region_37.38 | all-reduce | flops 1920 | bytes 15360 | tf_op jit(solution)/shard_map/psum | solution.py:230
  (387 shorter events, 83.4 us)
Async XLA Ops:
  7.2 209.7 %copy-start = (f32[768,512]{1,0:T(8,128)S(1)}, f32[768,512]{1,0:T(8,128)}, u32[]{:S(2)}) copy-start(f32[768,512]{1,0:T(8,128)} %param.35) | copy-start | bytes 4718596
  7.2 93.0 %all-gather.6.cloned.1.call-start = ((), (), s32[]{:S(2)}) async-start(), calls=%async_computation | async-start | bytes 1474560 | tf_op jit(solution)/shard_map/all_gather | solution.py:39
  8.0 207.5 %all-reduce.5.cloned.1.call-start = ((), (), s32[]{:S(2)}) async-start(), calls=%async_computation.1 | async-start | bytes 393216 | tf_op jit(solution)/shard_map/psum | solution.py:43
  14.8 39.1 %copy-start.107 = (bf16[768]{0:T(1024)(128)(2,1)S(1)}, bf16[768]{0:T(1024)(128)(2,1)}, u32[]{:S(2)}) copy-start(bf16[768]{0:T(1024)(128)(2,1)} %param.30) | copy-start | bytes 4612
  14.9 39.1 %copy-start.108 = (bf16[768]{0:T(1024)(128)(2,1)S(1)}, bf16[768]{0:T(1024)(128)(2,1)}, u32[]{:S(2)}) copy-start(bf16[768]{0:T(1024)(128)(2,1)} %param.28) | copy-start | bytes 4612
  14.9 39.1 %copy-start.109 = (bf16[768]{0:T(1024)(128)(2,1)S(1)}, bf16[768]{0:T(1024)(128)(2,1)}, u32[]{:S(2)}) copy-start(bf16[768]{0:T(1024)(128)(2,1)} %param.27) | copy-start | bytes 4612
  20.2 42.8 %slice-start = ((bf16[16,52,768]{2,0,1:T(8,128)(2,1)}), bf16[16,1,768]{2,0,1:T(8,128)(2,1)S(1)}, s32[]{:S(2)}) async-start(bf16[16,52,768]{2,0,1:T(8,128)(2,1)} %param.20), calls=%async_computation.4 | async-start | bytes 49152 | tf_op jit(solution)/shard_map/slice | solution.py:119
  54.0 48.4 %copy-start.66 = (f32[768]{0:T(1024)}, f32[768]{0:T(1024)S(1)}, u32[]{:S(2)}) copy-start(f32[768]{0:T(1024)S(1)} %convert_element_type.231) | copy-start | bytes 9220
  54.0 48.4 %copy-start.59 = (f32[768]{0:T(1024)}, f32[768]{0:T(1024)S(1)}, u32[]{:S(2)}) copy-start(f32[768]{0:T(1024)S(1)} %convert_element_type.229) | copy-start | bytes 9220
  104.6 133.1 %all-gather.8.cloned.1.call-start = ((), (), s32[]{:S(2)}) async-start(), calls=%async_computation.2 | async-start | bytes 1720320 | tf_op jit(solution)/shard_map/all_gather | solution.py:135
  108.4 41.9 %copy-start.19 = (f32[48,512]{1,0:T(8,128)S(1)}, f32[48,512]{1,0:T(8,128)}, u32[]{:S(2)}) copy-start(f32[48,512]{1,0:T(8,128)} %param.36) | copy-start | bytes 294916
  110.0 106.9 %copy-start.48 = (f32[768]{0:T(1024)S(1)}, f32[768]{0:T(1024)}, u32[]{:S(2)}) copy-start(f32[768]{0:T(1024)} %param.33) | copy-start | bytes 9220
  110.6 103.5 %copy-start.99 = (f32[48]{0:T(128)S(1)}, f32[48]{0:T(128)}, u32[]{:S(2)}) copy-start(f32[48]{0:T(128)} %get-tuple-element.46) | copy-start | bytes 580
  110.6 106.3 %copy-start.64 = (f32[768]{0:T(1024)S(1)}, f32[768]{0:T(1024)}, u32[]{:S(2)}) copy-start(f32[768]{0:T(1024)} %param.34) | copy-start | bytes 9220
  111.6 179.9 %all-reduce.7.cloned.1.call-start = ((), (), s32[]{:S(2)}) async-start(), calls=%async_computation.3 | async-start | bytes 2949120 | tf_op jit(solution)/shard_map/psum | solution.py:43
  150.5 65.0 %copy-start.88 = (f32[48]{0:T(128)}, f32[48]{0:T(128)S(1)}, u32[]{:S(2)}) copy-start(f32[48]{0:T(128)S(1)} %add_rsqrt_fusion.3) | copy-start | bytes 580
  250.6 40.9 %copy-start.76 = (f32[128]{0:T(128)S(1)}, f32[128]{0:T(128)}, u32[]{:S(2)}) copy-start(f32[128]{0:T(128)} %copy-done.75) | copy-start | bytes 1540
  250.6 40.9 %copy-start.81 = (f32[128]{0:T(128)S(1)}, f32[128]{0:T(128)}, u32[]{:S(2)}) copy-start(f32[128]{0:T(128)} %copy-done.80) | copy-start | bytes 1540
  253.6 43.1 %copy-start.47 = (bf16[16,192]{1,0:T(8,128)(2,1)S(1)}, bf16[16,192]{1,0:T(8,128)(2,1)}, u32[]{:S(2)}) copy-start(bf16[16,192]{1,0:T(8,128)(2,1)} %copy-done.46) | copy-start | bytes 18436
  253.6 43.1 %copy-start.52 = (s32[192]{0:T(256)S(1)}, s32[192]{0:T(256)}, u32[]{:S(2)}) copy-start(s32[192]{0:T(256)} %copy-done.51) | copy-start | bytes 2308
  335.3 63.1 %copy-start.39 = (bf16[128,192]{1,0:T(8,128)(2,1)S(1)}, bf16[128,192]{1,0:T(8,128)(2,1)}, u32[]{:S(2)}) copy-start(bf16[128,192]{1,0:T(8,128)(2,1)} %copy-done.38) | copy-start | bytes 147460
  336.2 63.3 %copy-start.4 = (f32[832,768]{1,0:T(8,128)S(1)}, f32[832,768]{1,0:T(8,128)}, u32[]{:S(2)}) copy-start(f32[832,768]{1,0:T(8,128)} %copy-done.3) | copy-start | bytes 7667716
  336.2 63.3 %copy-start.25 = (bf16[832,768]{1,0:T(8,128)(2,1)S(1)}, bf16[832,768]{1,0:T(8,128)(2,1)}, u32[]{:S(2)}) copy-start(bf16[832,768]{1,0:T(8,128)(2,1)} %get-tuple-element.40) | copy-start | bytes 3833860
  336.3 63.3 %copy-start.58 = (f32[768]{0:T(1024)S(1)}, f32[768]{0:T(1024)}, u32[]{:S(2)}) copy-start(f32[768]{0:T(1024)} %copy-done.57) | copy-start | bytes 9220
  (99 other events, 705.8 us)
Sparse Core Ops, SparseCore 0:
  9.6 20.1 all-gather.5
  104.8 32.5 all-reduce.4
  139.6 18.5 all-gather.7
  249.0 42.4 all-reduce.6

commit v2 on v1

v2 whole, which is shorter than its diff:
```python
import functools

import jax
import jax.numpy as jnp
from jax import lax
from jax.experimental import pallas as pl
from jax.experimental.pallas import tpu as pltpu
from jax.sharding import PartitionSpec as P

HEAD_DIM = 64
HIGH = lax.Precision.HIGHEST
F32 = jnp.float32
BF16 = jnp.bfloat16
MESH = pl.DeviceIdType.MESH
LOW = -1e30

G1, B1, G2, B2, OUTB, FC2B, PG, PB, FC1B, QB, VB, SCALE = range(12)
(LOSS, DG1, DB1, DQB, DVB, DOUTB, DG2, DB2, DFC1B, DFC2B, DPG, DPB) = range(12)


def norm_rows(values, gain, shift):
    centre = values - jnp.mean(values, -1, keepdims=True)
    spread = lax.rsqrt(jnp.mean(centre * centre, -1, keepdims=True) + 1e-05)
    scaled = centre * spread
    return (scaled * gain + shift, scaled, spread)


def norm_back(upper, gain, scaled, spread):
    inner = upper * gain
    return spread * (
        inner
        - jnp.mean(inner, -1, keepdims=True)
        - scaled * jnp.mean(inner * scaled, -1, keepdims=True)
    )


def dot(a, b, ca=1, cb=0, precision=None):
    return lax.dot_general(
        a, b, (((ca,), (cb,)), ((), ())), precision=precision, preferred_element_type=F32
    )


def iota(shape, dim):
    return lax.broadcasted_iota(jnp.int32, shape, dim)


def loop(count, step):
    if count == 1:
        step(0)
    else:
        lax.fori_loop(0, count, lambda i, c: (step(i), c)[1], 0)


def rows_at(index, size):
    if isinstance(index, int):
        return pl.ds(index * size, size)
    return pl.ds(pl.multiple_of(index * size, size), size)


class Plan:
    def __init__(self, mesh_sizes, images, w_qkv, w_fc1, w_proj, captions, positives):
        self.dps, self.mps = mesh_sizes
        self.group, self.seq, self.width = images.shape
        self.rows = self.group * self.seq
        self.local = w_qkv.shape[2]
        self.heads = self.local // HEAD_DIM
        self.hg = self.heads * self.group
        self.hidden = w_fc1.shape[1]
        self.emb = w_proj.shape[1]
        self.images = self.group * self.dps
        self.own = captions.shape[0]
        self.captions = self.own * self.dps
        self.places = positives.shape[1]
        self.block = min(128, self.images)
        self.blocks = self.images // self.block
        self.part = self.images // self.mps
        self.quarter = self.rows // self.mps

    def operands(self):
        r, d, loc, hid = self.rows, self.width, self.local, self.hidden
        return dict(
            x_in=((r, d), BF16),
            vec_in=((16, d), F32),
            plan_in=((self.group, 128), F32),
            wt_in=((3 * loc, d), BF16),
            wo_in=((loc, d), BF16),
            w1_in=((d, hid), BF16),
            w2_in=((hid, d), BF16),
            wp_in=((d, self.emb), F32),
            cap_in=((self.own, self.emb), F32),
        )

    def results(self):
        n, d, loc, hid = self.images, self.width, self.local, self.hidden
        return dict(
            block_out=((self.rows, d), BF16),
            images_out=((self.rows, d), F32),
            small_out=((16, d), F32),
            cap_out=((self.own, self.emb), F32),
            post_out=((n, d), F32),
            demb_out=((n, self.emb), F32),
            act_out=((n, hid), BF16),
            dy_out=((n, d), BF16),
            mlp_out=((n, d), BF16),
            dpre_out=((n, hid), BF16),
            ctx_out=((n, loc), BF16),
            dmid_out=((n, d), BF16),
            a_out=((self.dps * self.hg, d), BF16),
            b_out=((self.dps * self.hg, d), BF16),
            dq_out=((n, loc), BF16),
            dctx_out=((n, loc), BF16),
            xc_out=((n, d), BF16),
        )

    def scratch(self):
        r, d, loc, hid = self.rows, self.width, self.local, self.hidden
        n, m, hg, b = self.images, self.mps, self.hg, self.block
        return dict(
            x=((r, d), BF16),
            vec=((16, d), F32),
            wt=((3 * loc, d), BF16),
            w1=((d, hid), BF16),
            w2=((hid, d), BF16),
            wp=((d, self.emb), F32),
            cap=((self.own, self.emb), F32),
            wo=((m * loc, d), BF16),
            wod=((m * 128, d), BF16),
            attn=((r, d), BF16),
            q=((r, loc), BF16),
            k=((r, loc), BF16),
            v=((r, loc), BF16),
            q0=((r, 128), F32),
            q1=((r, 128), F32),
            k0=((r, 128), F32),
            k1=((r, 128), F32),
            v0=((r, 128), F32),
            v1=((r, 128), F32),
            c0=((r, 128), F32),
            c1=((r, 128), F32),
            qp=((128, 256), F32),
            kp=((128, 256), F32),
            vp=((128, 256), F32),
            probs=((hg, r), F32),
            plow=((hg, r), BF16),
            ca=((m, r, 128), BF16),
            cb=((m, r // 2, 128), BF16),
            mid=((r, d), F32),
            part=((r, d), BF16),
            half=((r // 2, d), BF16),
            send=((r // m, d), BF16),
            quart=((r // m, d), BF16),
            blk=((r, d), BF16),
            xc=((n, d), BF16),
            plan=((n, 128), F32),
            text=((self.captions, self.emb), BF16),
            cg=((m, n, loc), BF16),
            midc=((n, d), F32),
            mlp=((b, d), BF16),
            pre=((n, hid), F32),
            act=((b, hid), BF16),
            part1=((n, d), BF16),
            sum1=((m, n // m, d), BF16),
            all1=((n, d), BF16),
            part2=((n, d), BF16),
            sum2=((m, n // m, d), BF16),
            all2=((n, d), BF16),
            post=((b, d), F32),
            unit=((n, self.emb), F32),
            stat=((n, 2), F32),
            low=((n, self.emb), BF16),
            lg=((b, self.captions), F32),
            dtext=((self.own, self.emb), F32),
            arow=((hg, d), BF16),
            brow=((hg, d), BF16),
            crow=((8, self.captions), F32),
            demb=((b, self.emb), F32),
            dy=((b, d), BF16),
            dpre=((b, hid), BF16),
            dmid=((n, d), F32),
            dmidl=((b, d), BF16),
            dctx=((n, loc), BF16),
            capg=((self.own, self.emb), F32),
            small=((16, d), F32),
            dq=((n, loc), BF16),
            u=((m * 2 * hg, d), BF16),
            uq=((m * self.group, d), BF16),
            coef=((m * 2 * hg, 128), BF16),
            dattn=((r, d), F32),
            tot=((self.dps * 24, 128), F32),
        )


def kernel(plan, *refs):
    names = [*plan.operands(), *plan.results(), *plan.scratch()]
    sems = refs[len(names)]
    used = iter(range(256))

    def sem():
        return sems.at[next(used)]

    R = dict(zip(names, refs))
    rows, width, local, heads = plan.rows, plan.width, plan.local, plan.heads
    group, hg, dps, mps = plan.group, plan.hg, plan.dps, plan.mps
    dp, mp = lax.axis_index("dp"), lax.axis_index("mp")
    low_bit, high_bit = lax.rem(mp, 2), lax.div(mp, 2)
    near = mp + 1 - 2 * low_bit
    far = lax.rem(mp + 2, 4)
    ends = []
    put_sem = {n: sem() for n in ("mlp", "act", "post", "demb", "dy", "dpre", "dmidl")}

    def load(src, dst):
        copy = pltpu.make_async_copy(src, dst, sem())
        copy.start()
        return copy

    def store(name, dst=None):
        copy = pltpu.make_async_copy(R[name], R[dst or name + "_out"], sem())
        copy.start()
        ends.append(copy.wait)

    def put(name, i, value):
        R[name][...] = value
        copy = pltpu.make_async_copy(
            R[name], R[name.removesuffix("l") + "_out"].at[rows_at(i, plan.block)], put_sem[name]
        )
        copy.start()
        if plan.blocks == 1:
            ends.append(copy.wait)
        else:
            copy.wait()

    def send(src, dst, dp_to, mp_to, out, into):
        return pltpu.make_async_remote_copy(
            src_ref=src,
            dst_ref=dst,
            send_sem=out,
            recv_sem=into,
            device_id=(dp_to, mp_to),
            device_id_type=MESH,
        )

    class GatherDp:
        def __init__(self, buf, size, source=None):
            self.buf, self.size, self.source = buf, size, source
            self.out, self.into = sem(), sem()

        def start(self):
            mine = self.buf.at[rows_at(dp, self.size)]
            source = mine if self.source is None else self.source

            def one(i):
                to = lax.rem(dp + 1 + i, dps)
                send(source, mine, to, mp, self.out, self.into).start()

            loop(dps - 1, one)
            rest = self.buf.at[pl.ds(0, (dps - 1) * self.size)]
            self.all = send(rest, rest, dp, near, self.out, self.into)
            ends.append(self.all.wait_send)

        def wait(self):
            self.all.wait_recv()

    class GatherMp:
        def __init__(self, slot):
            self.slot = slot
            self.to_near = send(slot(mp), slot(mp), dp, near, sem(), sem())
            self.to_far = send(slot(mp), slot(mp), dp, far, sem(), sem())
            self.pass_on = send(slot(far), slot(far), dp, near, sem(), sem())

        def start(self):
            self.to_far.start()
            self.to_near.start()
            ends.extend([self.to_near.wait_send, self.to_far.wait_send])

        def forward(self):
            self.to_far.wait_recv()
            self.pass_on.start()
            ends.append(self.pass_on.wait_send)

        def wait(self):
            self.to_near.wait_recv()
            self.pass_on.wait_recv()

    class SumMp:
        def __init__(self, part, slots, total):
            self.part, self.slots, self.total = part, slots, total
            self.peers = [lax.rem(mp + i, mps) for i in (2, 3, 1)]
            self.out, self.into, self.back, self.done = sem(), sem(), sem(), sem()

        def start(self):
            for to in self.peers:
                send(
                    self.part.at[rows_at(to, plan.part)],
                    self.slots.at[mp],
                    dp,
                    to,
                    self.out,
                    self.into,
                ).start()
            self.slots[mp] = self.part[rows_at(mp, plan.part), :]
            three = self.slots.at[pl.ds(0, mps - 1)]
            self.first = send(three, three, dp, near, self.out, self.into)
            ends.append(self.first.wait_send)

        def turn(self):
            self.first.wait_recv()
            total = self.slots[0].astype(F32)
            for i in range(1, mps):
                total += self.slots[i].astype(F32)
            mine = rows_at(mp, plan.part)
            self.total[mine, :] = total.astype(BF16)
            for to in self.peers:
                send(
                    self.total.at[mine], self.total.at[mine], dp, to, self.back, self.done
                ).start()
            three = self.total.at[pl.ds(0, (mps - 1) * plan.part)]
            self.second = send(three, three, dp, near, self.back, self.done)
            ends.append(self.second.wait_send)

        def wait(self):
            self.second.wait_recv()

    barrier = pltpu.get_barrier_semaphore()

    def greet(i):
        pl.semaphore_signal(
            barrier, inc=1, device_id=(lax.rem(dp + 1 + i, dps), mp), device_id_type=MESH
        )

    loop(dps - 1, greet)
    for i in range(1, mps):
        pl.semaphore_signal(
            barrier, inc=1, device_id=(dp, lax.rem(mp + i, mps)), device_id_type=MESH
        )
    vec = R["vec"]
    got_vec = load(R["vec_in"], vec)
    got_x = load(R["x_in"], R["x"])
    got_wt = load(R["wt_in"], R["wt"])
    got_cls = load(
        R["x_in"].at[pl.ds(0, group)], R["xc"].at[rows_at(dp, group)]
    )
    got_plan = load(R["plan_in"], R["plan"].at[rows_at(dp, group)])
    got_wo = load(R["wo_in"], R["wo"].at[rows_at(mp, local)])
    got_cap = load(R["cap_in"], R["cap"])
    got_w1 = load(R["w1_in"], R["w1"])
    got_w2 = load(R["w2_in"], R["w2"])
    got_wp = load(R["wp_in"], R["wp"])
    R["small"][...] = jnp.zeros_like(R["small"])
    R["crow"][...] = jnp.zeros_like(R["crow"])
    R["dtext"][...] = jnp.zeros_like(R["dtext"])
    R["qp"][...] = jnp.zeros_like(R["qp"])
    R["kp"][...] = jnp.zeros_like(R["kp"])
    R["vp"][...] = jnp.zeros_like(R["vp"])
    for name in ("q1", "k1", "v1"):
        R[name][...] = jnp.zeros_like(R[name])
    got_vec.wait()
    got_x.wait()

    def row(i, size=width):
        return vec[i : i + 1, 0:size]

    def first_norm(i):
        at = rows_at(i, 64)
        normed = norm_rows(R["x"][at, :].astype(F32), row(G1), row(B1))[0]
        R["attn"][at, :] = normed.astype(BF16)

    loop(rows // 64, first_norm)
    pl.semaphore_wait(barrier, dps - 1 + mps - 1)
    got_wo.wait()
    gather_wo = GatherMp(lambda i: R["wo"].at[rows_at(i, local)])
    gather_wo.start()
    got_cls.wait()
    gather_xc = GatherDp(R["xc"], group)
    gather_xc.start()
    got_plan.wait()
    gather_plan = GatherDp(R["plan"], group)
    gather_plan.start()
    got_wt.wait()

    def project(i):
        at = rows_at(i, plan.quarter)
        a = R["attn"][at, :]
        for j, (name, shift) in enumerate((("q", QB), ("k", None), ("v", VB))):
            t = dot(a, R["wt"][j * local : (j + 1) * local, :], 1, 1)
            if shift is not None:
                t = t + row(shift, local)
            t = t.astype(BF16)
            R[name][at, :] = t
            t = t.astype(F32)
            R[name + "0"][at, :] = t[:, 0:128]
            R[name + "1"][at, 0 : local - 128] = t[:, 128:local]

    loop(mps, project)

    lane_head = iota((hg, local), 1) // HEAD_DIM
    own_head = lane_head == iota((hg, local), 0) // group

    def spread_heads(t):
        wide = jnp.concatenate([t.astype(F32)] * heads, 0)
        return jnp.where(own_head, wide, 0.0).astype(BF16)

    def join_heads(t):
        t = jnp.where(own_head, t, 0.0)
        total = t[0:group]
        for h in range(1, heads):
            total = total + t[h * group : (h + 1) * group]
        return total

    same = lax.rem(iota((hg, rows), 0), group) == lax.rem(iota((hg, rows), 1), group)
    qx = spread_heads(R["q"][0:group, :])
    scores = jnp.where(same, dot(qx, R["k"][...], 1, 1) * 0.125, LOW)
    weights = jnp.exp(scores - jnp.max(scores, -1, keepdims=True))
    probs = weights / jnp.sum(weights, -1, keepdims=True)
    R["probs"][...] = probs
    R["plow"][...] = probs.astype(BF16)
    mine = rows_at(dp, group)
    ctx = join_heads(dot(R["plow"][...], R["v"][...])).astype(BF16)
    cg = R["cg"].at[mp]
    cg[mine, :] = ctx
    gather_ctx = GatherDp(cg, group)
    gather_ctx.start()
    got_cap.wait()
    cap = R["cap"][...]
    cap_factor = lax.rsqrt(jnp.sum(cap * cap, -1, keepdims=True) + 1e-06)
    R["text"][rows_at(dp, plan.own), :] = (cap * cap_factor).astype(BF16)
    gather_text = GatherDp(R["text"], plan.own)
    gather_text.start()
    gather_wo.forward()

    def attend(t):
        for j in range(2):
            at = pl.ds(2 * t + j, plan.seq, stride=group)
            for name in "qkv":
                for i in range(2):
                    into = R[name + "p"].at[j * 64 : j * 64 + plan.seq, i * 128 : i * 128 + 128]
                    into[...] = R[name + str(i)][at, :]
        qb = R["qp"][...].astype(BF16)
        kb, vb = R["kp"][...], R["vp"][...]
        head_of = iota((128, 256), 1) // HEAD_DIM
        r, c = iota((128, 128), 0), iota((128, 128), 1)
        seen = (r // 64 == c // 64) & (lax.rem(c, 64) < plan.seq)
        total = jnp.zeros((128, 256), F32)
        for h in range(heads):
            kh = jnp.where(head_of == h, kb, 0.0).astype(BF16)
            vh = jnp.where(head_of == h, vb, 0.0).astype(BF16)
            s = jnp.where(seen, dot(qb, kh, 1, 1) * 0.125, LOW)
            e = jnp.exp(s - jnp.max(s, -1, keepdims=True))
            p = (e / jnp.sum(e, -1, keepdims=True)).astype(BF16)
            total += dot(p, vh)
        for j in range(2):
            at = pl.ds(2 * t + j, plan.seq, stride=group)
            for i in range(2):
                R["c" + str(i)][at, :] = total[
                    j * 64 : j * 64 + plan.seq, i * 128 : i * 128 + 128
                ]

    loop(group // 2, attend)
    R["ca"][mp] = R["c0"][...].astype(BF16)
    R["cb"][mp] = jnp.concatenate(
        [R["c1"][0 : rows // 2, 0:64], R["c1"][rows // 2 : rows, 0:64]], 1
    ).astype(BF16)

    gather_ctx.wait()
    gather_cg = GatherMp(lambda i: R["cg"].at[i])
    gather_cg.start()
    gather_ca = GatherMp(lambda i: R["ca"].at[i])
    gather_cb = GatherMp(lambda i: R["cb"].at[i])
    gather_ca.start()
    gather_cb.start()

    R["brow"][...] = dot(R["plow"][...], R["attn"][...]).astype(BF16)
    gather_b = GatherDp(R["b_out"], hg, R["brow"])
    gather_b.start()
    ends.append(load(R["brow"], R["b_out"].at[rows_at(dp, hg)]).wait)

    gather_cg.forward()
    gather_wo.wait()
    for m in range(mps):
        tail = R["wo"][m * local + 128 : (m + 1) * local, :]
        R["wod"][m * 128 : (m + 1) * 128, :] = jnp.concatenate([tail, tail], 0)
    gather_xc.wait()
    got_w1.wait()
    got_w2.wait()
    gather_cg.wait()

    def class_forward(i):
        at = rows_at(i, plan.block)
        total = R["xc"][at, :].astype(F32) + row(OUTB)
        for m in range(mps):
            total += dot(R["cg"][m, at, :], R["wo"][m * local : (m + 1) * local, :])
        R["midc"][at, :] = total
        mlp = norm_rows(total, row(G2), row(B2))[0].astype(BF16)
        put("mlp", i, mlp)
        pre = dot(mlp, R["w1"][...]) + row(FC1B, plan.hidden)
        R["pre"][at, :] = pre
        act = (pre * jax.nn.sigmoid(1.702 * pre)).astype(BF16)
        put("act", i, act)
        R["part1"][at, :] = dot(act, R["w2"][...]).astype(BF16)

    loop(plan.blocks, class_forward)
    sum1 = SumMp(R["part1"], R["sum1"], R["all1"])
    sum1.start()
    store("xc")

    size = plan.quarter

    def bulk(index):
        at = rows_at(index, size)
        side = lax.div(index, 2)
        at_half = rows_at(lax.rem(index, 2), size)
        total = R["x"][at, :].astype(F32) + row(OUTB)
        keep = iota((size, 128), 1) // HEAD_DIM == side
        for m in range(mps):
            total += dot(R["ca"][m, at, :], R["wo"][m * local : m * local + 128, :])
            tail = jnp.where(keep, R["cb"][m, at_half, :].astype(F32), 0.0).astype(BF16)
            total += dot(tail, R["wod"][m * 128 : (m + 1) * 128, :])
        R["mid"][at, :] = total
        mlp = norm_rows(total, row(G2), row(B2))[0].astype(BF16)
        pre = dot(mlp, R["w1"][...]) + row(FC1B, plan.hidden)
        act = (pre * jax.nn.sigmoid(1.702 * pre)).astype(BF16)
        R["part"][at, :] = dot(act, R["w2"][...]).astype(BF16)

    q_near_far = 2 * (1 - low_bit) + 1 - high_bit
    q_near = 2 * (1 - low_bit) + high_bit
    q_far = 2 * low_bit + 1 - high_bit
    q_own = 2 * low_bit + high_bit

    def to_near(index, slot):
        move = send(
            R["part"].at[rows_at(index, size)],
            R["half"].at[pl.ds(slot * size, size)],
            dp,
            near,
            sem(),
            sem(),
        )
        move.start()
        ends.append(move.wait_send)
        return move

    gather_ca.forward()
    gather_cb.forward()
    gather_ca.wait()
    gather_cb.wait()
    bulk(q_near_far)
    half0 = to_near(q_near_far, 0)
    sum1.turn()
    bulk(q_near)
    half1 = to_near(q_near, 1)
    gather_text.wait()
    gather_plan.wait()
    got_wp.wait()
    sum1.wait()

    scale = jnp.exp(row(SCALE, 1))
    crow = R["crow"]
    crow[0:1, :] = jnp.full((1, plan.captions), LOW, F32)

    def class_out(at):
        return R["midc"][at, :] + R["all1"][at, :].astype(F32) + row(FC2B)

    def logits_at(at):
        if plan.blocks == 1:
            return R["lg"][...]
        return scale * dot(R["low"][at, :], R["text"][...], 1, 1)

    def head(i):
        at = rows_at(i, plan.block)
        post = norm_rows(class_out(at), row(PG), row(PB))[0]
        put("post", i, post)
        emb = dot(post, R["wp"][...], precision=HIGH)
        factor = lax.rsqrt(jnp.sum(emb * emb, -1, keepdims=True) + 1e-06)
        R["stat"][at, 0:1] = factor
        unit = emb * factor
        R["unit"][at, :] = unit
        image_low = unit.astype(BF16)
        R["low"][at, :] = image_low
        logits = scale * dot(image_low, R["text"][...], 1, 1)
        R["lg"][...] = logits
        crow[0:1, :] = jnp.maximum(crow[0:1, :], jnp.max(logits, 0, keepdims=True))

    loop(plan.blocks, head)

    def matches(at):
        ids = iota((plan.block, plan.captions), 1).astype(F32)
        found = R["plan"][at, 0:1] == ids
        for place in range(1, plan.places):
            found |= R["plan"][at, place : place + 1] == ids
        return jnp.where(found, 1.0, 0.0)

    def put_small(i, value):
        R["small"][i : i + 1, 0 : value.shape[1]] += value

    half_i, half_c = 0.5 / plan.images, 0.5 / plan.captions

    def stats(i):
        at = rows_at(i, plan.block)
        logits = logits_at(at)
        matched = matches(at) * logits
        crow[1:2, :] += jnp.sum(jnp.exp(logits - crow[0:1, :]), 0, keepdims=True)
        crow[2:3, :] += jnp.sum(matched, 0, keepdims=True)
        top = jnp.max(logits, 1, keepdims=True)
        lse = top + jnp.log(jnp.sum(jnp.exp(logits - top), 1, keepdims=True))
        R["stat"][at, 1:2] = lse
        counts = R["plan"][at, plan.places : plan.places + 1]
        terms = lse - jnp.sum(matched, 1, keepdims=True) / counts
        put_small(LOSS, half_i * jnp.sum(terms, 0, keepdims=True))

    loop(plan.blocks, stats)
    crow[3:4, :] = crow[0:1, :] + jnp.log(crow[1:2, :])
    put_small(LOSS, half_c * jnp.sum(crow[3:4, :] - crow[2:3, :], 1, keepdims=True))

    shape = (plan.captions, plan.own)
    own_captions = iota(shape, 0) == iota(shape, 1) + dp * plan.own
    own_captions = jnp.where(own_captions, 1.0, 0.0).astype(BF16)

    def head_back(i):
        at = rows_at(i, plan.block)
        logits = logits_at(at)
        match = matches(at)
        counts = R["plan"][at, plan.places : plan.places + 1]
        dlog = half_i * (jnp.exp(logits - R["stat"][at, 1:2]) - match / counts)
        dlog += half_c * (jnp.exp(logits - crow[3:4, :]) - match)
        dlow = dlog.astype(BF16)
        both = jnp.sum(dlow.astype(F32) * logits, 1, keepdims=True)
        R["small"][LOSS : LOSS + 1, 128:129] += jnp.sum(both, 0, keepdims=True)
        dimage = scale * dot(dlow, R["text"][...])
        own = dot(dlow, own_captions).astype(BF16)
        R["dtext"][...] += dot(own, R["low"][at, :], 0, 0)
        unit = R["unit"][at, :]
        demb = R["stat"][at, 0:1] * (dimage - unit * jnp.sum(unit * dimage, -1, keepdims=True))
        put("demb", i, demb)
        dpost = dot(demb, R["wp"][...], 1, 1, HIGH)
        _, hat, spread = norm_rows(class_out(at), row(PG), row(PB))
        dcls = norm_back(dpost, row(PG), hat, spread)
        put_small(DPG, jnp.sum(dpost * hat, 0, keepdims=True))
        put_small(DPB, jnp.sum(dpost, 0, keepdims=True))
        put_small(DFC2B, jnp.sum(dcls, 0, keepdims=True))
        R["dmid"][at, :] = dcls
        dy = dcls.astype(BF16)
        put("dy", i, dy)
        pre = R["pre"][at, :]
        sigma = jax.nn.sigmoid(1.702 * pre)
        slope = sigma + 1.702 * pre * sigma * (1.0 - sigma)
        dpre = (dot(dy, R["w2"][...], 1, 1) * slope).astype(BF16)
        put("dpre", i, dpre)
        put_small(DFC1B, jnp.sum(dpre.astype(F32), 0, keepdims=True))
        R["part2"][at, :] = dot(dpre, R["w1"][...], 1, 1).astype(BF16)

    loop(plan.blocks, head_back)
    sum2 = SumMp(R["part2"], R["sum2"], R["all2"])
    sum2.start()
    dtext = scale * R["dtext"][...]
    text_unit = cap * cap_factor
    R["capg"][...] = cap_factor * (
        dtext - text_unit * jnp.sum(text_unit * dtext, -1, keepdims=True)
    )
    store("capg", "cap_out")

    bulk(q_far)
    half0.wait_recv()
    R["send"][...] = (
        R["part"][rows_at(q_far, size), :].astype(F32) + R["half"][0:size, :].astype(F32)
    ).astype(BF16)
    to_far = send(R["send"], R["quart"], dp, far, sem(), sem())
    to_far.start()
    ends.append(to_far.wait_send)
    sum2.turn()
    bulk(q_own)
    half1.wait_recv()
    sum2.wait()

    def class_back(i):
        at = rows_at(i, plan.block)
        dmlp = R["all2"][at, :].astype(F32)
        _, hat, spread = norm_rows(R["midc"][at, :], row(G2), row(B2))
        dmid = R["dmid"][at, :] + norm_back(dmlp, row(G2), hat, spread)
        put_small(DG2, jnp.sum(dmlp * hat, 0, keepdims=True))
        put_small(DB2, jnp.sum(dmlp, 0, keepdims=True))
        put_small(DOUTB, jnp.sum(dmid, 0, keepdims=True))
        R["dmid"][at, :] = dmid
        dlow = dmid.astype(BF16)
        put("dmidl", i, dlow)
        R["dctx"][at, :] = dot(dlow, R["wo"][rows_at(mp, local), :], 1, 1).astype(BF16)

    loop(plan.blocks, class_back)
    store("dctx")

    dx = spread_heads(R["dctx"][mine, :])
    qx = spread_heads(R["q"][0:group, :])
    probs = R["probs"][...]
    dprobs = dot(dx, R["v"][...], 1, 1)
    dscores = probs * (dprobs - jnp.sum(probs * dprobs, -1, keepdims=True))
    dscores = (dscores * 0.125).astype(BF16)
    dq = join_heads(dot(dscores, R["k"][...])).astype(BF16)
    R["dq"][mine, :] = dq
    R["arow"][...] = dot(dscores, R["attn"][...]).astype(BF16)
    gather_a = GatherDp(R["a_out"], hg, R["arow"])
    R["uq"][rows_at(mp, group), :] = dot(dq, R["wt"][0:local, :]).astype(BF16)
    uk = dot(qx, R["wt"][local : 2 * local, :])
    uv = dot(dx, R["wt"][2 * local : 3 * local, :])
    u_at = rows_at(mp, 2 * hg)
    R["u"][u_at, :] = jnp.concatenate([uk, uv], 0).astype(BF16)
    fold = jnp.where(
        iota((rows, 128), 0) // group == iota((rows, 128), 1), 1.0, 0.0
    ).astype(BF16)
    coef = jnp.concatenate([dot(dscores, fold), dot(R["plow"][...], fold)], 0)
    R["coef"][u_at, :] = coef.astype(BF16)
    gather_coef = GatherMp(lambda i: R["coef"].at[rows_at(i, 2 * hg)])
    gather_uq = GatherMp(lambda i: R["uq"].at[rows_at(i, group)])
    gather_u = GatherMp(lambda i: R["u"].at[rows_at(i, 2 * hg)])
    for g in (gather_coef, gather_uq, gather_u):
        g.start()
    gather_a.start()
    ends.append(load(R["arow"], R["a_out"].at[rows_at(dp, hg)]).wait)
    gather_dq = GatherDp(R["dq"], group)
    gather_dq.start()

    to_far.wait_recv()
    at = rows_at(q_own, size)
    quarter = R["part"][at, :].astype(F32) + R["half"][size : 2 * size, :].astype(F32)
    quarter += R["quart"][...].astype(F32)
    R["blk"][at, :] = (R["mid"][at, :] + quarter + row(FC2B)).astype(BF16)
    for g in (gather_coef, gather_uq, gather_u):
        g.forward()
    blk = R["blk"]
    blk_far = send(blk.at[at], blk.at[at], dp, far, sem(), sem())
    blk_far.start()
    for g in (gather_coef, gather_uq, gather_u):
        g.wait()

    def spread_coef(i):
        at = rows_at(i, size)
        pick = jnp.where(
            (iota((size, 128), 0) + i * size) // group == iota((size, 128), 1), 1.0, 0.0
        ).astype(BF16)
        wide = dot(pick, R["coef"][...], 1, 1)
        shape = wide.shape
        fits = lax.rem(iota(shape, 0), group) == lax.rem(iota(shape, 1), group)
        R["dattn"][at, :] = dot(jnp.where(fits, wide, 0.0).astype(BF16), R["u"][...])

    loop(mps, spread_coef)
    total = R["uq"][0:group, :].astype(F32)
    for m in range(1, mps):
        total += R["uq"][m * group : (m + 1) * group, :].astype(F32)
    R["dattn"][0:group, :] += total

    def first_back(i):
        at = rows_at(i, 64)
        upper = R["dattn"][at, :]
        _, hat, spread = norm_rows(R["x"][at, :].astype(F32), row(G1), row(B1))
        R["dattn"][at, :] = norm_back(upper, row(G1), hat, spread)
        put_small(DG1, jnp.sum(upper * hat, 0, keepdims=True))
        put_small(DB1, jnp.sum(upper, 0, keepdims=True))

    loop(rows // 64, first_back)
    R["dattn"][0:group, :] += R["dmid"][mine, :]
    store("dattn", "images_out")

    put_small(DQB, jnp.sum(dq.astype(F32), 0, keepdims=True))
    prob_sum = jnp.sum(R["plow"][...].astype(F32), -1, keepdims=True)
    put_small(DVB, jnp.sum(dx.astype(F32) * prob_sum, 0, keepdims=True))
    spans = []
    for i, count in ((DG1, width), (DB1, width), (DQB, local), (DVB, local)):
        spans += [(i, c, min(128, count - c)) for c in range(0, count, 128)]
    mine24 = pl.multiple_of(dp * 24, 8)
    R["tot"][pl.ds(mine24, 24), :] = jnp.zeros((24, 128), F32)
    for n, (i, c, size_c) in enumerate(spans):
        R["tot"][pl.ds(mine24 + n, 1), 0:size_c] = R["small"][i : i + 1, c : c + size_c]
    gather_tot = GatherDp(R["tot"], 24)
    gather_tot.start()
    blk_far.wait()
    both = blk.at[rows_at(low_bit, 2 * size)]
    blk_near = send(both, both, dp, near, sem(), sem())
    blk_near.start()
    gather_tot.wait()

    def add_up(i):
        for n, (j, c, size_c) in enumerate(spans):
            value = R["tot"][pl.ds(i * 24 + n, 1), 0:size_c]
            R["small"][j : j + 1, c : c + size_c] += value

    for i in (DG1, DB1, DQB, DVB):
        R["small"][i : i + 1, :] = jnp.zeros((1, width), F32)
    loop(dps, add_up)
    store("small")
    gather_dq.wait()
    store("dq")
    store_ctx = pltpu.make_async_copy(cg, R["ctx_out"], sem())
    store_ctx.start()
    ends.append(store_ctx.wait)
    gather_b.wait()
    blk_near.wait()
    store("blk", "block_out")
    gather_a.wait()
    for end in ends:
        end()


def run_kernel(plan, *operands):
    anywhere = pl.BlockSpec(memory_space=pl.ANY)
    return pl.pallas_call(
        functools.partial(kernel, plan),
        out_shape=[jax.ShapeDtypeStruct(s, t) for s, t in plan.results().values()],
        in_specs=[anywhere] * len(plan.operands()),
        out_specs=[anywhere] * len(plan.results()),
        scratch_shapes=[pltpu.VMEM(s, t) for s, t in plan.scratch().values()]
        + [pltpu.SemaphoreType.DMA((160,))],
        compiler_params=pltpu.CompilerParams(
            collective_id=0, has_side_effects=True, vmem_limit_bytes=61 << 20
        ),
    )(*operands)


def body(
    images,
    ln1_gain,
    ln1_bias,
    w_qkv,
    qv_bias,
    w_out,
    out_bias,
    ln2_gain,
    ln2_bias,
    w_fc1,
    fc1_bias,
    w_fc2,
    fc2_bias,
    post_gain,
    post_bias,
    w_proj,
    captions,
    logit_scale,
    caption_counts,
    positives,
):
    sizes = (lax.axis_size("dp"), lax.axis_size("mp"))
    plan = Plan(sizes, images, w_qkv, w_fc1, w_proj, captions, positives)
    width, local, group, heads = plan.width, plan.local, plan.group, plan.heads

    x = jnp.transpose(images, (1, 0, 2)).reshape(plan.rows, width)
    wt = jnp.transpose(w_qkv, (1, 2, 0)).reshape(3 * local, width)

    def fit(t):
        t = t.astype(F32)
        return jnp.pad(t, (0, width - t.shape[0]))

    vectors = (
        *(ln1_gain, ln1_bias, ln2_gain, ln2_bias, out_bias, fc2_bias, post_gain, post_bias),
        *(fc1_bias, qv_bias[0], qv_bias[1], logit_scale),
    )
    vec = jnp.stack([fit(t) for t in vectors] + [jnp.zeros((width,), F32)] * 4)
    table = jnp.concatenate([positives, caption_counts[:, None]], 1).astype(F32)
    table = jnp.pad(table, ((0, 0), (0, 128 - table.shape[1])))
    got = run_kernel(plan, x, vec, table, wt, w_out, w_fc1, w_fc2, w_proj, captions)
    R = dict(zip(plan.results(), got))

    hg = plan.hg
    lane_head = iota((heads, group, local), 2) // HEAD_DIM
    own_head = lane_head == iota((heads, group, local), 0)

    def spread_heads(t):
        t = t.reshape(plan.dps, 1, group, local)
        return jnp.where(own_head[None], t, 0).reshape(plan.dps * hg, local)

    attn_cls = norm_rows(R["xc_out"].astype(F32), ln1_gain.astype(F32), ln1_bias.astype(F32))[0]
    attn_cls = attn_cls.astype(BF16)
    q_all = (dot(attn_cls, wt[:local], 1, 1) + qv_bias[0].astype(F32)).astype(BF16)
    wq_grad = dot(R["dq_out"], attn_cls, 0, 0)
    wk_grad = dot(spread_heads(q_all), R["a_out"], 0, 0)
    wv_grad = dot(spread_heads(R["dctx_out"]), R["b_out"], 0, 0)
    qkv_grad = jnp.concatenate([wq_grad, wk_grad, wv_grad], 0)
    small = R["small_out"]

    def as_images(t):
        return jnp.transpose(t.reshape(plan.seq, group, width), (1, 0, 2))

    return (
        small[LOSS, 0:1],
        as_images(R["block_out"]),
        as_images(R["images_out"]),
        small[DG1],
        small[DB1],
        jnp.transpose(qkv_grad.reshape(3, local, width), (2, 0, 1)),
        small[DQB : DVB + 1, :local],
        dot(R["ctx_out"], R["dmid_out"], 0, 0),
        small[DOUTB],
        small[DG2],
        small[DB2],
        dot(R["mlp_out"], R["dpre_out"], 0, 0),
        small[DFC1B],
        dot(R["act_out"], R["dy_out"], 0, 0),
        small[DFC2B],
        small[DPG],
        small[DPB],
        dot(R["post_out"], R["demb_out"], 0, 0, HIGH),
        R["cap_out"],
        small[LOSS, 128:129],
    )


def solution(mesh):
    full, per_dp = P(), P("dp")
    return jax.shard_map(
        body,
        mesh=mesh,
        in_specs=(
            P("dp", None, None),
            full,
            full,
            P(None, None, "mp"),
            P(None, "mp"),
            P("mp", None),
            full,
            full,
            full,
            P(None, "mp"),
            P("mp"),
            P("mp", None),
            full,
            full,
            full,
            full,
            P("dp", None),
            full,
            per_dp,
            P("dp", None),
        ),
        out_specs=(
            full,
            P("dp", None, None),
            P("dp", None, None),
            full,
            full,
            P(None, None, "mp"),
            P(None, "mp"),
            P("mp", None),
            full,
            full,
            full,
            P(None, "mp"),
            P("mp"),
            P("mp", None),
            full,
            full,
            full,
            full,
            P("dp", None),
            full,
        ),
        check_vma=False,
    )
```

time: 517 us -> 114 us (0.22)
  blocking collectives: 343 us -> 0 us
  Pallas kernels: 0 us -> 76.6 us
  matrix products: 57.1 us -> 9.88 us
  waiting for transfers between devices: 36.5 us -> 0 us
  other arithmetic: 42.1 us -> 5.94 us
  between operations: 20.3 us -> 1.53 us
    all_gather x13 -> x0, blocking collectives: 306 us -> none  [the longest x9 282 us: gather_dp(): return lax.all_gather(x, 'dp', axis=0, tiled=True)]
    pallas_call x0 -> x1, Pallas kernels: none -> 76.6 us  [run_kernel(): pl.pallas_call(functools.partial(kernel, plan), out_shape=[jax.ShapeDtype...]
    dot_general x34 -> x8, matrix products: 46.9 us -> 9.88 us  [dot(): lax.dot_general(a, b, (((ca,), (cb,)), ((), ())), precision=precision, pr...]
    psum x1 -> x0, blocking collectives: 37 us -> none  [body(): lax.psum((jnp.sum(dattn * xhat, 0), jnp.sum(dattn, 0), jnp.stack([jnp.sum...]
    psum x2 -> x0, waiting for transfers between devices: 35.8 us -> none  [sum_mp(): return lax.psum(x, 'mp')]
    reduce_sum x21 -> x0, other arithmetic: 18.7 us -> none  [the longest x3 5.4 us: body(): jnp.sum(dattn, 0)]
    dot_general x2 -> x0, matrix products: 7.52 us -> none  [the longest x1 3.85 us: body(): jnp.einsum('ghqe,ghke->ghqk', grouped(q), grouped(k), preferred_element_t...]
    another operation x0 -> x14, local copies, waits for them, and re-layouts: none -> 7.48 us  [body(): vec = jnp.stack([fit(t) for t in vectors] + [jnp.zeros((width,), F32)] * 4)]
  transfers between devices with their start and end apart: 4 -> 0, of which waited for: 1 -> 0; matrix products, arithmetic and copies ran while one was open for 12% -> 0% of each run, Pallas kernels for 0% -> 0%
where the time goes in v2:
time: 114 us; the launch traced here: 113 us
  Pallas kernels  76.6 us (67%)
  local copies, waits for them, and re-layouts  19 us (17%)
  matrix products  9.88 us (9%)
  other arithmetic  5.94 us (5%)
  between operations  1.53 us (1%)
    pallas_call x1, Pallas kernels, run_kernel(): pl.pallas_call(functools.partial(kernel, plan), out_shape=[jax.ShapeDtype...  76.6 us
    dot_general x8, matrix products, dot(): lax.dot_general(a, b, (((ca,), (cb,)), ((), ())), precision=precision, pr...  9.88 us
    another operation x14, local copies, waits for them, and re-layouts, body(): vec = jnp.stack([fit(t) for t in vectors] + [jnp.zeros((width,), F32)] * 4)  7.48 us
    unnamed x34, local copies, waits for them, and re-layouts  5.11 us

profile of v2, /device:TPU:0, one launch (start us, length us, event | category | flops | bytes accessed | tf_op | source)
XLA Modules:
  0.0 112.9 jit_solution(11715348441542767289)
XLA Ops:
  1.3 0.8 slice_reduce_fusion.9
  2.1 0.7 reshape.100
  5.5 0.7 stack.73
  6.2 0.7 stack.74
  8.3 0.7 convert_element_type.45
  9.7 0.7 copy.44
  10.4 0.8 copy.43
  11.9 1.3 %stack.83.refs_1_ = f32[16,768]{1,0:T(8,128)} concatenate(f32[1,768]{1,0:T(1,128)S(1)} %stack.63, f32[1,768]{1,0:T(1,128)S(1)} %stack.64, f32[1,768]{1,0:T(1,128)S(1)} %reshape.98, f32[1,768]{1,0:T(1,128)S(1)} %reshape.99, f32[1,768]{1,0:T(1,128)S(1)} %reshape.100, f32[1,768]{1,0:T(1,128)S(1)} %reshape.101, f32[1,768]{1,0:T(1,128)S(1)} %stack.73, f32[1,768]{1,0:T(1,128)S(1)} %stack.74, ...), dimensions={0} | concatenate | bytes 98304 | tf_op jit(solution)/shard_map/stack | solution.py:852
  13.2 76.6 %shard_map.347 = (bf16[832,768]{1,0:T(8,128)(2,1)}, f32[832,768]{1,0:T(8,128)}, f32[16,768]{1,0:T(8,128)}, f32[48,512]{1,0:T(8,128)}, f32[128,768]{1,0:T(8,128)}...) custom-call(bf16[832,768]{1,0:T(8,128)(2,1)} %bitcast.41, ...), custom_call_target="tpu_custom_call" | custom-call | tf_op jit(solution)/shard_map/pallas_call | solution.py:802
  89.8 1.1 convert_reduce_fusion
  91.0 1.1 fusion.3
  92.1 1.2 %fusion.10 = (f32[1,1]{1,0:T(1,128)}, f32[1,1]{1,0:T(1,128)}) fusion(f32[16,768]{1,0:T(8,128)} %get-tuple-element.37), kind=kLoop, calls=%fused_computation.37 | loop fusion | bytes 16 | tf_op jit(solution)/shard_map/slice | solution.py:898
  93.3 1.3 %slice.56 = f32[2,192]{1,0:T(2,128)} slice(f32[16,768]{1,0:T(8,128)} %get-tuple-element.37), slice={[3:5], [0:192]} | slice | bytes 3072 | tf_op jit(solution)/shard_map/slice | solution.py:885
  94.6 1.7 %slice_reduce_fusion = (f32[768]{0:T(1024)}, f32[768]{0:T(1024)}, f32[768]{0:T(1024)}, f32[768]{0:T(1024)}, f32[768]{0:T(1024)}, /*index=5*/f32[768]{0:T(1024)}, f32[768]{0:T(1024)}, f32[768]{0:T(1024)}, f32[768]{0:T(1024)}) fusion(f32[16,768]{1,0:T(8,128)} %get-tuple-element.37), kind=kLoop, calls=%fused_computation.16 | loop fusion | bytes 55296 | tf_op jit(solution)/shard_map/slice | solution.py:895
  96.3 1.4 %fusion = bf16[128,192]{0,1:T(8,128)(2,1)S(1)} fusion(bf16[3,192,768]{2,1,0:T(8,128)(2,1)} %bitcast.43, f32[192]{0:T(256)S(1)} %add.44, bf16[128,768]{1,0:T(8,128)(2,1)} %get-tuple-element.41, f32[768]{0:T(1024)S(1)} %convert_element_type.46, f32[768]{0:T(1024)S(1)} %convert_element_type.45, f32[128]{0:T(128)S(1)} %add_rsqrt_fusion, ...), kind=kOutput, calls=%fused_computation.2 | convolution fusion | flops 38387712 | bytes 548608 | tf_op jit(solution)/shard_map/dot_general | solution.py:38
  97.8 0.9 broadcast_select_fusion.1
  99.8 1.3 %pad_maximum_fusion = f32[576,768]{1,0:T(8,128)} fusion(f32[192,768]{1,0:T(8,128)S(1)} %fusion.12, f32[192,768]{1,0:T(8,128)S(1)} %fusion.11, f32[192,768]{1,0:T(8,128)S(1)} %fusion.8), kind=kLoop, calls=%fused_computation | loop fusion | flops 884736 | bytes 3538944 | tf_op jit(solution)/shard_map/concatenate | solution.py:872
  101.1 1.1 fusion.13
  102.2 2.6 %fusion.16 = f32[768,512]{1,0:T(8,128)} fusion(f32[128,768]{1,0:T(8,128)S(1)} %copy-done.5, f32[128,512]{1,0:T(8,128)S(1)} %copy-done.6), kind=kOutput, calls=%fused_computation.43 | convolution fusion | flops 603979776 | bytes 2228224 | tf_op jit(solution)/shard_map/dot_general | solution.py:38
  104.8 1.9 %fusion.14 = f32[768,768]{1,0:T(8,128)} fusion(bf16[128,768]{1,0:T(8,128)(2,1)S(1)} %copy-done.10, bf16[128,768]{1,0:T(8,128)(2,1)S(1)} %copy-done.11), kind=kOutput, calls=%fused_computation.41 | convolution fusion | flops 150994944 | bytes 2752512 | tf_op jit(solution)/shard_map/dot_general | solution.py:38
  106.7 1.9 %fusion.15 = f32[768,768]{1,0:T(8,128)} fusion(bf16[128,768]{1,0:T(8,128)(2,1)S(1)} %copy-done.8, bf16[128,768]{1,0:T(8,128)(2,1)S(1)} %copy-done.9), kind=kOutput, calls=%fused_computation.42 | convolution fusion | flops 150994944 | bytes 2752512 | tf_op jit(solution)/shard_map/dot_general | solution.py:38
  108.6 1.0 copy.50
  109.7 1.1 %copy-done = f32[832,768]{1,0:T(8,128)S(1)} copy-done((f32[832,768]{1,0:T(8,128)S(1)}, f32[832,768]{1,0:T(8,128)}, u32[]{:S(2)}) %copy-start) | copy-done | bytes 2555928
  110.8 1.5 %copy.51 = f32[16,52,768]{2,0,1:T(8,128)} copy(f32[16,52,768]{2,0,1:T(8,128)S(1)} %bitcast.38) | data formatting | bytes 5111808
  (55 shorter events, 7.4 us)
Async XLA Ops:
  89.8 8.9 %copy-start.4 = (bf16[384,768]{1,0:T(8,128)(2,1)S(1)}, bf16[384,768]{1,0:T(8,128)(2,1)}, u32[]{:S(2)}) copy-start(bf16[384,768]{1,0:T(8,128)(2,1)} %get-tuple-element.42) | copy-start | bytes 1769476
  89.8 9.2 %copy-start.3 = (bf16[384,768]{1,0:T(8,128)(2,1)S(1)}, bf16[384,768]{1,0:T(8,128)(2,1)}, u32[]{:S(2)}) copy-start(bf16[384,768]{1,0:T(8,128)(2,1)} %get-tuple-element.44) | copy-start | bytes 1769476
  97.7 1.7 %copy-start.1 = (bf16[128,768]{1,0:T(8,128)(2,1)S(1)}, bf16[128,768]{1,0:T(8,128)(2,1)}, u32[]{:S(2)}) copy-start(bf16[128,768]{1,0:T(8,128)(2,1)} %get-tuple-element.41) | copy-start | bytes 589828
  97.7 1.7 %copy-start.14 = (bf16[128,192]{1,0:T(8,128)(2,1)S(1)}, bf16[128,192]{1,0:T(8,128)(2,1)}, u32[]{:S(2)}) copy-start(bf16[128,192]{1,0:T(8,128)(2,1)} %get-tuple-element.40) | copy-start | bytes 147460
  99.8 1.4 %copy-start.7 = (bf16[128,768]{1,0:T(8,128)(2,1)S(1)}, bf16[128,768]{1,0:T(8,128)(2,1)}, u32[]{:S(2)}) copy-start(bf16[128,768]{1,0:T(8,128)(2,1)} %get-tuple-element.46) | copy-start | bytes 589828
  99.8 1.4 %copy-start.13 = (bf16[128,192]{1,0:T(8,128)(2,1)S(1)}, bf16[128,192]{1,0:T(8,128)(2,1)}, u32[]{:S(2)}) copy-start(bf16[128,192]{1,0:T(8,128)(2,1)} %get-tuple-element.45) | copy-start | bytes 147460
  99.8 2.4 %copy-start.5 = (f32[128,768]{1,0:T(8,128)S(1)}, f32[128,768]{1,0:T(8,128)}, u32[]{:S(2)}) copy-start(f32[128,768]{1,0:T(8,128)} %get-tuple-element.51) | copy-start | bytes 1179652
  99.8 2.4 %copy-start.6 = (f32[128,512]{1,0:T(8,128)S(1)}, f32[128,512]{1,0:T(8,128)}, u32[]{:S(2)}) copy-start(f32[128,512]{1,0:T(8,128)} %get-tuple-element.52) | copy-start | bytes 786436
  101.1 3.7 %copy-start.10 = (bf16[128,768]{1,0:T(8,128)(2,1)S(1)}, bf16[128,768]{1,0:T(8,128)(2,1)}, u32[]{:S(2)}) copy-start(bf16[128,768]{1,0:T(8,128)(2,1)} %get-tuple-element.47) | copy-start | bytes 589828
  101.1 3.7 %copy-start.11 = (bf16[128,768]{1,0:T(8,128)(2,1)S(1)}, bf16[128,768]{1,0:T(8,128)(2,1)}, u32[]{:S(2)}) copy-start(bf16[128,768]{1,0:T(8,128)(2,1)} %get-tuple-element.48) | copy-start | bytes 589828
  104.8 1.9 %copy-start.8 = (bf16[128,768]{1,0:T(8,128)(2,1)S(1)}, bf16[128,768]{1,0:T(8,128)(2,1)}, u32[]{:S(2)}) copy-start(bf16[128,768]{1,0:T(8,128)(2,1)} %get-tuple-element.49) | copy-start | bytes 589828
  104.8 1.9 %copy-start.9 = (bf16[128,768]{1,0:T(8,128)(2,1)S(1)}, bf16[128,768]{1,0:T(8,128)(2,1)}, u32[]{:S(2)}) copy-start(bf16[128,768]{1,0:T(8,128)(2,1)} %get-tuple-element.50) | copy-start | bytes 589828
  106.7 1.9 %copy-start.2 = (bf16[832,768]{1,0:T(8,128)(2,1)S(1)}, bf16[832,768]{1,0:T(8,128)(2,1)}, u32[]{:S(2)}) copy-start(bf16[832,768]{1,0:T(8,128)(2,1)} %get-tuple-element.38) | copy-start | bytes 3833860
  108.6 2.2 %copy-start = (f32[832,768]{1,0:T(8,128)S(1)}, f32[832,768]{1,0:T(8,128)}, u32[]{:S(2)}) copy-start(f32[832,768]{1,0:T(8,128)} %get-tuple-element.39) | copy-start | bytes 7667716
  110.8 1.5 %copy-start.12 = (f32[48,512]{1,0:T(8,128)S(1)}, f32[48,512]{1,0:T(8,128)}, u32[]{:S(2)}) copy-start(f32[48,512]{1,0:T(8,128)} %get-tuple-element.111) | copy-start | bytes 294916
